TPU v7x, 32 devices: a whole 2x2x4 slice. The times are simulated.
32 devices in a mesh: section: 2 (over core), table: 16 (over z, y, x).
Axes of the slice: x: 2, y: 2, z: 4, core: 2. Of those that a mesh axis runs over, the one named last changes fastest.
Arguments:
- gate_a: bfloat16 [2, 1024, 4096], P('section', 'table'), may hold values from -6 to 6
- cotangent_a: bfloat16 [2, 1024, 4096], P('section', 'table'), may hold values from -6 to 6
- gate_b: bfloat16 [2, 1024, 4096], P('section', 'table'), may hold values from -6 to 6
- table: bfloat16 [1024, 4096], P('table'), may hold values from -6 to 6
- row_ids: int32 [2, 2, 16, 128], P('section', None, 'table'), may hold values from 0 to 1023, as said below
- slots: int32 [2, 2, 1024, 128], P('section', None, 'table'), may hold values from 0 to 127, as said below
- weights: float32 [2, 2, 1024, 128], P('section', None, 'table'), may hold values from 0.02 to 0.2
Outputs:
- mixed_b: bfloat16 [2, 1024, 4096], P('section', 'table')
- grad_gate_a: bfloat16 [2, 1024, 4096], P('section', 'table')
- grad_weights_a: float32 [2, 1024, 128], P('section', 'table')
- grad_table: float32 [1024, 4096], P('table', 'section')
Inputs may be any that keep to these rules, and one draw needn't show every extreme that they name: `row_ids`: row r is held by index r // 64 of table. The 128 ids of one list are distinct, and at most 8 of them are held by one index of table; in every section and micro-batch some index of table holds 8 ids of every device's list. `slots`: the 32 picks of one token and head are distinct, and every position of a device's list is picked by some token of that device and micro-batch.
All inputs are finite; a program needn't handle non-finite values.
Results may differ from a plain program's by a relative error of at most 0.0057.
Values may be sent and summed in bfloat16 or wider, within the bound.
A program may use at most 128 MiB of HBM per device.

v0:
```python
import jax
import jax.numpy as jnp
from jax import lax
from jax.experimental import pallas as pl
from jax.experimental.pallas import tpu as pltpu
from jax.sharding import PartitionSpec as P

ROW_LIMIT = 8
CHUNK = 512
GROUP = 8
MESH = pl.DeviceIdType.MESH


def mix_picks(slot_rows, weight_rows):
    picks = slot_rows.shape[1]
    lane = lax.broadcasted_iota(jnp.int32, slot_rows.shape, 1)

    def group(_, carry):
        slot, weight, total = carry
        for p in range(GROUP):
            hit = slot[:, p : p + 1] == lane
            total = total + jnp.where(hit, weight[:, p : p + 1], 0.0)
        return (
            pltpu.roll(slot, picks - GROUP, 1), pltpu.roll(weight, picks - GROUP, 1), total
        )

    start = (slot_rows, weight_rows, jnp.zeros(weight_rows.shape, jnp.float32))
    return lax.fori_loop(0, picks // GROUP, group, start)[2].astype(jnp.bfloat16)


def place_rows(ids, owners, rows_dev, lanes, base):
    listed = ids.shape[1]
    f32, bf16 = jnp.float32, jnp.bfloat16
    owner = lax.broadcasted_iota(jnp.int32, (owners, listed), 0)
    first = owner * rows_dev
    member = ((ids >= first) & (ids < first + rows_dev)).astype(f32)
    before = lax.broadcasted_iota(jnp.int32, (listed, listed), 0) < lax.broadcasted_iota(
        jnp.int32, (listed, listed), 1
    )
    earlier = jnp.dot(
        member.astype(bf16), before.astype(f32).astype(bf16), preferred_element_type=f32
    )
    spot = earlier + (owner * (2 * ROW_LIMIT) + base).astype(f32)
    place = jnp.sum(member * spot, axis=0, keepdims=True).astype(jnp.int32)
    offset = ids - jnp.sum(member * first.astype(f32), axis=0, keepdims=True).astype(jnp.int32)
    space = lax.broadcasted_iota(jnp.int32, (owners * 2 * ROW_LIMIT, listed), 0)
    wide = (space == place).astype(f32).astype(bf16)
    row = lax.broadcasted_iota(jnp.int32, (lanes, listed), 0)
    held = (row == offset).astype(f32).astype(bf16)
    ask = lax.dot_general(wide, held, (((1,), (1,)), ((), ())), preferred_element_type=f32)
    return wide, ask


def spread(mixing, wide):
    return lax.dot_general(
        mixing, wide, (((1,), (1,)), ((), ())), preferred_element_type=jnp.float32
    ).astype(jnp.bfloat16)


def drain(block, sem):
    pltpu.make_async_copy(block, block, sem).wait()


def exchange(
    gate_a, cot_a, gate_b, table, row_ids, slots, weights,
    mixed_b, grad_gate, grad_weights, grad_table,
    asks, mix_a, asked, rows_out, fetched, grads_out, arrived, grad_memory, scores,
    table_far, asked_far,
    ask_send, ask_recv, grad_send, grad_recv, row_send, row_recv,
    table_send, table_recv, far_send, far_recv,
):
    sections = lax.axis_size("section")
    owners = lax.axis_size("table")
    sec = lax.axis_index("section")
    me = lax.axis_index("table")
    rows_dev, features = table.shape
    part = features // sections
    everyone = sections * owners
    mine = sec * owners + me
    half = owners // 2
    seat = lax.rem(me, half)
    low = me - seat
    twin = lax.rem(me + half, owners)
    f32 = jnp.float32

    def peers(step, first):
        @pl.loop(first, everyone)
        def _(hop):
            over = lax.rem(mine + hop, everyone)
            step(over // owners, lax.rem(over, owners))

    barrier = pltpu.get_barrier_semaphore()
    peers(
        lambda s, t: pl.semaphore_signal(
            barrier, inc=1, device_id={"section": s, "table": t}, device_id_type=MESH
        ),
        1,
    )

    lanes = asks.shape[-1]
    ids = row_ids[...]
    wide_a, ask_a = place_rows(ids[0:1], owners, rows_dev, lanes, 0)
    wide_b, ask_b = place_rows(ids[1:2], owners, rows_dev, lanes, ROW_LIMIT)
    asks[...] = (ask_a + ask_b).astype(jnp.bfloat16).reshape(asks.shape)
    pl.semaphore_wait(barrier, everyone - 1)

    def remote(source, target, send, recv, s, t):
        pltpu.make_async_remote_copy(
            src_ref=source, dst_ref=target, send_sem=send, recv_sem=recv,
            device_id={"section": s, "table": t}, device_id_type=MESH,
        ).start()

    peers(lambda s, t: remote(asks.at[t], asked.at[mine], ask_send, ask_recv, s, t), 1)
    pltpu.make_async_copy(asks.at[me], asked.at[mine], ask_recv).start()

    @pl.loop(1, half)
    def _(hop):
        t = low + lax.rem(seat + hop, half)
        other = lax.rem(t + half, owners)
        remote(asks.at[other], asked_far.at[seat], far_send, far_recv, sec, t)

    pltpu.make_async_copy(asks.at[twin], asked_far.at[seat], far_recv).start()
    remote(table, table_far, table_send, table_recv, sec, twin)
    mix_a[...] = spread(mix_picks(slots[0], weights[0]), wide_a)

    @pl.loop(0, features // CHUNK)
    def _(c):
        cols = pl.ds(pl.multiple_of(c * CHUNK, CHUNK), CHUNK)
        gate = gate_a[:, cols].astype(f32)
        value = (cot_a[:, cols].astype(f32) * gate * jax.nn.sigmoid(gate)).astype(jnp.bfloat16)
        grad_memory[:, cols] = value
        rows = lax.dot_general(
            mix_a[...], value, (((0,), (0,)), ((), ())), preferred_element_type=f32
        ).reshape(owners, 2, ROW_LIMIT, CHUNK)[:, 0]
        per = part // CHUNK
        inner = pl.ds(pl.multiple_of(lax.rem(c, per) * CHUNK, CHUNK), CHUNK)
        grads_out[c // per, :, :, inner] = rows.astype(jnp.bfloat16)

    peers(
        lambda s, t: remote(grads_out.at[s, t], arrived.at[mine], grad_send, grad_recv, s, t), 1
    )
    pltpu.make_async_copy(grads_out.at[sec, me], arrived.at[mine], grad_recv).start()

    drain(asked, ask_recv)
    drain(asked_far, far_recv)

    def serve(wanted, rows_ref, side, place):
        wanted = wanted.reshape(half * 2 * ROW_LIMIT, -1)[:, :rows_dev]

        @pl.loop(0, features // CHUNK)
        def _(c):
            cols = pl.ds(pl.multiple_of(c * CHUNK, CHUNK), CHUNK)
            rows = jnp.dot(wanted, rows_ref[:, cols], preferred_element_type=f32)
            rows = rows.astype(jnp.bfloat16).reshape(half, 2 * ROW_LIMIT, CHUNK)
            rows_out[side, :, :, cols] = rows

        @pl.loop(1, half)
        def _(hop):
            spot = lax.rem(seat + hop, half)
            remote(
                rows_out.at[side, spot], fetched.at[place], row_send, row_recv, sec, low + spot
            )

        pltpu.make_async_copy(rows_out.at[side, seat], fetched.at[place], row_recv).start()

    serve(asked[pl.ds(sec * owners + low, half)], table, 0, me)
    drain(table_far, table_recv)
    serve(asked_far[...], table_far, 1, twin)

    mix_b = spread(mix_picks(slots[1], weights[1]), wide_b)
    asked_a = asked[...].astype(f32)[:, :ROW_LIMIT].reshape(everyone * ROW_LIMIT, -1)
    asked_a = asked_a.astype(jnp.bfloat16)
    drain(arrived, grad_recv)

    @pl.loop(0, part // CHUNK)
    def _(c):
        cols = pl.ds(pl.multiple_of(c * CHUNK, CHUNK), CHUNK)
        block = arrived[:, :, cols].reshape(everyone * ROW_LIMIT, CHUNK)
        total = lax.dot_general(
            asked_a, block, (((0,), (0,)), ((), ())), preferred_element_type=f32
        )
        grad_table[:, cols] = total[:rows_dev]

    drain(fetched, row_recv)
    scores[...] = jnp.zeros_like(scores)

    @pl.loop(0, features // CHUNK)
    def _(c):
        cols = pl.ds(pl.multiple_of(c * CHUNK, CHUNK), CHUNK)
        rows = fetched[:, :, cols].reshape(owners * 2 * ROW_LIMIT, CHUNK)
        memory = jnp.dot(mix_a[...], rows, preferred_element_type=f32)
        gate = gate_a[:, cols].astype(f32)
        sig = jax.nn.sigmoid(gate)
        incoming = cot_a[:, cols].astype(f32)
        grad_gate[:, cols] = (incoming * memory * sig * (1.0 + gate * (1.0 - sig))).astype(
            jnp.bfloat16
        )
        scores[...] += lax.dot_general(
            grad_memory[:, cols], rows, (((1,), (1,)), ((), ())), preferred_element_type=f32
        )
        memory = jnp.dot(mix_b, rows, preferred_element_type=f32)
        gate = gate_b[:, cols].astype(f32)
        mixed_b[:, cols] = (gate * jax.nn.sigmoid(gate) * memory).astype(jnp.bfloat16)

    listed = lax.dot_general(
        scores[...], wide_a.astype(f32), (((1,), (0,)), ((), ())),
        precision=lax.Precision.HIGHEST, preferred_element_type=f32,
    )
    grad_weights[...] = jnp.take_along_axis(listed, slots[0], axis=1)
    drain(asked.at[pl.ds(0, everyone - 1)], ask_send)
    drain(arrived.at[pl.ds(0, everyone - 1)], grad_send)
    drain(rows_out.at[:, pl.ds(0, half - 1)], row_send)
    drain(asked_far.at[pl.ds(0, half - 1)], far_send)
    drain(table_far, table_send)


def local(gate_a, cotangent_a, gate_b, table, row_ids, slots, weights):
    owners = lax.axis_size("table")
    sections = lax.axis_size("section")
    rows_dev, features = table.shape
    tokens = gate_a.shape[1]
    listed = row_ids.shape[-1]
    part = features // sections
    lanes = -(-rows_dev // 128) * 128
    bf16 = jnp.bfloat16
    everyone = sections * owners
    vmem = pl.BlockSpec(memory_space=pltpu.VMEM)
    mixed_b, grad_gate, grad_weights, grad_table = pl.pallas_call(
        exchange,
        out_shape=(
            jax.ShapeDtypeStruct((tokens, features), bf16),
            jax.ShapeDtypeStruct((tokens, features), bf16),
            jax.ShapeDtypeStruct((tokens, listed), jnp.float32),
            jax.ShapeDtypeStruct((rows_dev, part), jnp.float32),
        ),
        in_specs=[vmem] * 7,
        out_specs=(vmem,) * 4,
        scratch_shapes=[
            pltpu.VMEM((owners, 2 * ROW_LIMIT, lanes), bf16),
            pltpu.VMEM((tokens, owners * 2 * ROW_LIMIT), bf16),
            pltpu.VMEM((everyone, 2 * ROW_LIMIT, lanes), bf16),
            pltpu.VMEM((2, owners // 2, 2 * ROW_LIMIT, features), bf16),
            pltpu.VMEM((owners, 2 * ROW_LIMIT, features), bf16),
            pltpu.VMEM((sections, owners, ROW_LIMIT, part), bf16),
            pltpu.VMEM((everyone, ROW_LIMIT, part), bf16),
            pltpu.VMEM((tokens, features), bf16),
            pltpu.VMEM((tokens, owners * 2 * ROW_LIMIT), jnp.float32),
            pltpu.VMEM((rows_dev, features), bf16),
            pltpu.VMEM((owners // 2, 2 * ROW_LIMIT, lanes), bf16),
        ]
        + [pltpu.SemaphoreType.DMA] * 10,
        compiler_params=pltpu.CompilerParams(
            collective_id=0, has_side_effects=True, vmem_limit_bytes=60 * 1024 * 1024
        ),
    )(
        gate_a[0], cotangent_a[0], gate_b[0], table, row_ids[0, :, 0], slots[0], weights[0]
    )
    return mixed_b[None], grad_gate[None], grad_weights[None], grad_table


def solution(mesh):
    return jax.shard_map(
        local,
        mesh=mesh,
        in_specs=(
            P("section", "table", None),
            P("section", "table", None),
            P("section", "table", None),
            P("table", None),
            P("section", None, "table", None),
            P("section", None, "table", None),
            P("section", None, "table", None),
        ),
        out_specs=(
            P("section", "table", None),
            P("section", "table", None),
            P("section", "table", None),
            P("table", "section"),
        ),
        check_vma=False,
    )
```

profile of v0, /device:TPU:7, one launch (start us, length us, event | category | flops | bytes accessed | tf_op | source)
XLA Modules:
  0.0 80.9 jit_solution(9933850001445303103)
XLA Ops:
  0.6 76.2 %shard_map.102 = (bf16[64,4096]{1,0:T(8,128)(2,1)}, bf16[64,4096]{1,0:T(8,128)(2,1)}, f32[64,128]{1,0:T(8,128)}, f32[64,2048]{1,0:T(8,128)}) custom-call(bf16[64,4096]{1,0:T(8,128)(2,1)} %bitcast.11, bf16[64,4096]{1,0:T(8,128)(2,1)} %bitcast.12, bf16[64,4096]{1,0:T(8,128)(2,1)} %bitcast.13, bf16[64,4096]{1,0:T(8,128)(2,1)} %table.1, s32[2,128]{1,0:T(2,128)} %bitcast.17, ...), custom_call_target="tpu_custom_call" | custom-call | tf_op jit(solution)/shard_map/pallas_call | solution.py:228
  76.8 0.0 copy-start.1
  76.8 1.9 %copy.15 = bf16[1,64,4096]{2,1,0:T(8,128)(2,1)} copy(bf16[1,64,4096]{2,1,0:T(8,128)(2,1)} %bitcast.10) | data formatting | bytes 1048576
  78.7 0.0 copy-done.1
  78.7 0.0 copy-start.2
  78.7 0.0 copy-start
  78.7 0.8 copy.16
  79.5 0.0 copy-done.2
  79.5 0.6 copy.17
  80.1 0.0 copy-done
  80.1 0.8 copy.18
Async XLA Ops:
  76.8 1.9 %copy-start.1 = (bf16[64,4096]{1,0:T(8,128)(2,1)S(1)}, bf16[64,4096]{1,0:T(8,128)(2,1)}, u32[]{:S(2)}) copy-start(bf16[64,4096]{1,0:T(8,128)(2,1)} %get-tuple-element.9) | copy-start | bytes 1572868
  78.7 0.8 copy-start.2
  78.7 1.4 %copy-start = (f32[64,2048]{1,0:T(8,128)S(1)}, f32[64,2048]{1,0:T(8,128)}, u32[]{:S(2)}) copy-start(f32[64,2048]{1,0:T(8,128)} %get-tuple-element.19) | copy-start | bytes 1572868
where the time goes:
time: 81.1 us; the launch traced here: 80.9 us
  Pallas kernels  76.2 us (94%)
  local copies, waits for them, and re-layouts  4.14 us (5%)
    pallas_call x1, Pallas kernels, local(): pl.pallas_call(exchange, out_shape=(jax.ShapeDtypeStruct((tokens, feature...  76.2 us
    unnamed x10, local copies, waits for them, and re-layouts  4.14 us

commit v1 on v0

v1 whole, which is shorter than its diff:
```python
import jax
import jax.numpy as jnp
from jax import lax
from jax.experimental import pallas as pl
from jax.experimental.pallas import tpu as pltpu
from jax.sharding import PartitionSpec as P

ROW_LIMIT = 8
CHUNK = 512
LAYERS = 4
PIECES = 4
UNROLL = 8
MESH = pl.DeviceIdType.MESH
BF16, F32 = jnp.bfloat16, jnp.float32


def iota(shape, axis):
    return lax.broadcasted_iota(jnp.int32, shape, axis)


def hot(mask):
    return mask.astype(F32).astype(BF16)


def contract(lhs, rhs, dims, **options):
    return lax.dot_general(lhs, rhs, (dims, ((), ())), preferred_element_type=F32, **options)


def locate(ids, owners, plane, rows_dev):
    listed = ids.shape[1]
    line = iota((owners, listed), 0)
    layer = line & (LAYERS - 1)
    column = lax.shift_right_logical(line, LAYERS.bit_length() - 1)
    first = (layer * plane + column) * rows_dev
    member = ((ids >= first) & (ids < first + rows_dev)).astype(F32)
    before = iota((listed, listed), 0) < iota((listed, listed), 1)
    earlier = contract(member.astype(BF16), hot(before), ((1,), (0,)))
    rank = jnp.sum(member * earlier, axis=0, keepdims=True).astype(jnp.int32)
    spot = jnp.sum(member * line.astype(F32), axis=0, keepdims=True).astype(jnp.int32)
    start = jnp.sum(member * first.astype(F32), axis=0, keepdims=True).astype(jnp.int32)
    held = (member * (ids - start + 1).astype(F32)).astype(BF16)
    return rank, spot, held


def mix_picks(slots_t, weights_t, listed):
    picks, tokens = slots_t.shape
    position = iota((listed, tokens), 0).astype(F32)

    def group(g, total):
        base = pl.multiple_of(g * UNROLL, UNROLL)
        slot = slots_t[pl.ds(base, UNROLL), :]
        weight = weights_t[pl.ds(base, UNROLL), :]
        for p in range(UNROLL):
            hit = slot[p : p + 1] == position
            total = total + jnp.where(hit, weight[p : p + 1], 0.0)
        return total

    start = jnp.zeros((listed, tokens), F32)
    return lax.fori_loop(0, picks // UNROLL, group, start)


def drain(block, sem):
    pltpu.make_async_copy(block, block, sem).wait()


def exchange(
    gate_a_in, cot_a_in, gate_b_in, table_in, row_ids, slots, weights,
    mixed_b, grad_gate, grad_weights, grad_table,
    gate_a, cot_a, gate_b, col, slots_t, weights_t, mix_wide, mix_tall, wide_list,
    message, asked, codes, grads_out, arrived, rows_out, fetched, grad_memory, scores,
    rs_out, rs_in,
    load, ask_send, ask_recv, tab_send, tab_recv, par_send, par_recv,
    grad_send, grad_recv, row_send, row_recv, rs_send, rs_recv,
):
    sections = lax.axis_size("section")
    owners = lax.axis_size("table")
    plane = owners // LAYERS
    rows_dev, features = table_in.shape
    tokens = gate_a.shape[0]
    listed = row_ids.shape[1]
    part = features // sections
    group = sections * plane
    width = codes.shape[2] - asked_width(group)
    piece = features // PIECES
    last = LAYERS - 1

    sec = lax.axis_index("section")
    me = lax.axis_index("table")
    z = me // plane
    p_me = lax.rem(me, plane)
    seat = sec * plane + p_me
    parity = lax.rem(sec, 2)
    partner = sec + 1 - 2 * parity
    step_z = 1 - 2 * parity
    ahead_ok = (z + step_z >= 0) & (z + step_z <= last)

    def peer(hop):
        if plane & (plane - 1):
            return lax.rem(p_me + hop, plane)
        other, bit = p_me, 1
        while bit < plane:
            if hop & bit:
                other = other + bit - 2 * bit * lax.rem(p_me // bit, 2)
            bit *= 2
        return other

    def other_section(hop):
        return lax.rem(sec + hop, sections)

    def at(layer, place):
        return layer * plane + place

    def greet(s, t):
        pl.semaphore_signal(
            pltpu.get_barrier_semaphore(), inc=1,
            device_id={"section": s, "table": t}, device_id_type=MESH,
        )

    def remote(source, target, send, recv, s, t):
        pltpu.make_async_remote_copy(
            src_ref=source, dst_ref=target, send_sem=send, recv_sem=recv,
            device_id={"section": s, "table": t}, device_id_type=MESH,
        ).start()

    for hop in range(plane):
        for turn in range(sections):
            if hop or turn:
                greet(other_section(turn), at(z, peer(hop)))

    @pl.when(z > 0)
    def _():
        greet(sec, at(z - 1, p_me))

    @pl.when(z < last)
    def _():
        greet(sec, at(z + 1, p_me))

    pltpu.make_async_copy(table_in, col.at[z], load.at[0]).start()
    pltpu.make_async_copy(gate_a_in, gate_a, load.at[1]).start()
    pltpu.make_async_copy(cot_a_in, cot_a, load.at[2]).start()
    pltpu.make_async_copy(gate_b_in, gate_b, load.at[3]).start()

    ids = row_ids[...]
    rank_a, spot_a, held_a = locate(ids[0:1], owners, plane, rows_dev)
    rank_b, spot_b, held_b = locate(ids[1:2], owners, plane, rows_dev)
    lane = iota((codes.shape[2], listed), 0)
    base = p_me * (2 * ROW_LIMIT)
    lanes_a = hot((lane == rank_a + base) | (lane == rank_a + (seat * ROW_LIMIT + width)))
    lanes_b = hot(lane == rank_b + (base + ROW_LIMIT))
    asking = contract(held_a, lanes_a, ((1,), (1,))) + contract(held_b, lanes_b, ((1,), (1,)))
    for q in range(plane):
        message[q] = asking[q * LAYERS : (q + 1) * LAYERS]

    signals = group - 1 + jnp.where(z > 0, 1, 0) + jnp.where(z < last, 1, 0)
    pl.semaphore_wait(pltpu.get_barrier_semaphore(), signals)

    drain(col.at[z], load.at[0])

    @pl.when(ahead_ok)
    def _():
        remote(col.at[z], col.at[z], tab_send, tab_recv.at[z], sec, at(z + step_z, p_me))

    for hop in range(plane):
        q = peer(hop)
        for turn in range(sections):
            if hop or turn:
                remote(
                    message.at[q], asked.at[seat], ask_send, ask_recv,
                    other_section(turn), at(z, q),
                )
    pltpu.make_async_copy(message.at[p_me], asked.at[seat], ask_recv).start()

    slots_t[...] = jnp.transpose(slots[...].reshape(2 * tokens, -1).astype(F32))
    weights_t[...] = jnp.transpose(weights[...].reshape(2 * tokens, -1))
    mixing_t = mix_picks(slots_t, weights_t, listed).astype(BF16)
    space = iota((owners * 2 * ROW_LIMIT, listed), 0)
    wide_a = hot(space == spot_a * (2 * ROW_LIMIT) + rank_a)
    wide_b = hot(space == spot_b * (2 * ROW_LIMIT) + (rank_b + ROW_LIMIT))
    tall_a = hot(iota((owners * ROW_LIMIT, listed), 0) == spot_a * ROW_LIMIT + rank_a)
    wide_list[...] = wide_a
    mix_tall[...] = contract(tall_a, mixing_t[:, :tokens], ((1,), (0,))).astype(BF16)

    drain(gate_a, load.at[1])
    drain(cot_a, load.at[2])
    for half in range(sections):

        @pl.loop(0, part // CHUNK)
        def _(c):
            inner = pl.ds(pl.multiple_of(c * CHUNK, CHUNK), CHUNK)
            cols = pl.ds(pl.multiple_of(half * part + c * CHUNK, CHUNK), CHUNK)
            gate = gate_a[:, cols].astype(F32)
            value = (cot_a[:, cols].astype(F32) * gate * jax.nn.sigmoid(gate)).astype(BF16)
            grad_memory[:, cols] = value
            rows = contract(mix_tall[...], value, ((1,), (0,))).astype(BF16)
            grads_out[half, :, :, :, inner] = rows.reshape(plane, LAYERS, ROW_LIMIT, CHUNK)

        for hop in range(1, plane):
            q = peer(hop)
            remote(
                grads_out.at[half, q], arrived.at[:, seat], grad_send, grad_recv, half, at(z, q)
            )

        @pl.when(sec == half)
        def _():
            pltpu.make_async_copy(
                grads_out.at[half, p_me], arrived.at[:, seat], grad_recv
            ).start()

        @pl.when(sec != half)
        def _():
            remote(
                grads_out.at[half, p_me], arrived.at[:, seat], grad_send, grad_recv, half, me
            )

    drain(asked, ask_recv)
    serving, summing = asked[sec * plane, :, :width], asked[0, :, width:]
    for q in range(1, plane):
        serving = serving + asked[sec * plane + q, :, :width]
    for q in range(1, group):
        summing = summing + asked[q, :, width:]
    for layer in range(LAYERS):
        codes[layer, :, :width] = serving[layer : layer + 1]
        codes[layer, :, width:] = summing[layer : layer + 1]

    def serve(layer):
        code = codes[layer, :, :width]
        pick = (iota((rows_dev, width), 0).astype(F32) == code - 1.0).astype(F32)
        pick = jnp.transpose(pick)[: plane * 2 * ROW_LIMIT].astype(BF16)
        for c in range(PIECES):
            for k in range(piece // CHUNK):
                cols = pl.ds(c * piece + k * CHUNK, CHUNK)
                rows = contract(pick, col[layer, :, cols], ((1,), (0,))).astype(BF16)
                rows_out[layer, :, :, cols] = rows.reshape(plane, 2 * ROW_LIMIT, CHUNK)
            cols = pl.ds(c * piece, piece)
            for hop in range(1, plane):
                q = peer(hop)
                remote(
                    rows_out.at[layer, q, :, cols], fetched.at[p_me, layer, :, cols],
                    row_send, row_recv.at[c], sec, at(z, q),
                )
            pltpu.make_async_copy(
                rows_out.at[layer, p_me, :, cols], fetched.at[p_me, layer, :, cols],
                row_recv.at[c],
            ).start()

    def summed(layer, cols):
        code = codes[layer, :, width:][:, : group * ROW_LIMIT]
        pick = hot(iota((rows_dev, group * ROW_LIMIT), 0).astype(F32) == code - 1.0)
        block = arrived[layer, :, :, cols].reshape(group * ROW_LIMIT, -1)
        return contract(pick, block, ((1,), (0,)))

    def table_hop(h):
        behind, ahead = z - step_z * h, z + step_z * h

        @pl.when((behind >= 0) & (behind <= last))
        def _():
            drain(col.at[behind], tab_recv.at[behind])

            @pl.when(ahead_ok)
            def _():
                remote(
                    col.at[behind], col.at[behind], tab_send, tab_recv.at[behind],
                    sec, at(z + step_z, p_me),
                )

            remote(col.at[behind], col.at[behind], par_send, par_recv.at[behind], partner, me)
            serve(behind)

        @pl.when((ahead >= 0) & (ahead <= last))
        def _():
            drain(col.at[ahead], par_recv.at[ahead])
            serve(ahead)

    def reduce_step(k):
        for way in range(2):
            place = z if way == 0 else last - z
            far = last - (k - place)
            layer = far if way == 0 else last - far
            target = z + 1 if way == 0 else z - 1

            def pass_on(earlier):
                @pl.loop(0, part // CHUNK)
                def _(c):
                    cols = pl.ds(pl.multiple_of(c * CHUNK, CHUNK), CHUNK)
                    total = summed(layer, cols)
                    if earlier:
                        total = total + rs_in[way, k - 1, :, cols].astype(F32)
                    rs_out[way, k, :, cols] = total.astype(BF16)

                remote(
                    rs_out.at[way, k], rs_in.at[way, k], rs_send, rs_recv.at[way, k],
                    sec, at(target, p_me),
                )

            @pl.when(place == 0)
            def _():
                pass_on(False)

            if k:

                @pl.when((place > 0) & (place <= k))
                def _():
                    drain(rs_in.at[way, k - 1], rs_recv.at[way, k - 1])
                    pass_on(True)

    serve(z)
    table_hop(1)

    mix_wide[:tokens] = contract(mixing_t[:, :tokens], wide_a, ((0,), (1,))).astype(BF16)
    mix_wide[tokens:] = contract(mixing_t[:, tokens:], wide_b, ((0,), (1,))).astype(BF16)
    scores[...] = jnp.zeros_like(scores)
    drain(arrived, grad_recv)

    for h in range(2, LAYERS):
        reduce_step(h - 2)
        table_hop(h)
    reduce_step(LAYERS - 2)

    drain(gate_b, load.at[3])
    for c in range(PIECES):
        drain(fetched.at[:, :, :, pl.ds(c * piece, piece)], row_recv.at[c])
        for k in range(piece // CHUNK):
            cols = pl.ds(c * piece + k * CHUNK, CHUNK)
            rows = fetched[:, :, :, cols].reshape(owners * 2 * ROW_LIMIT, CHUNK)
            memory = contract(mix_wide[...], rows, ((1,), (0,)))
            gate = gate_a[:, cols].astype(F32)
            sig = jax.nn.sigmoid(gate)
            incoming = cot_a[:, cols].astype(F32)
            grad_gate[:, cols] = (
                incoming * memory[:tokens] * sig * (1.0 + gate * (1.0 - sig))
            ).astype(BF16)
            scores[...] += contract(grad_memory[:, cols], rows, ((1,), (1,)))
            gate = gate_b[:, cols].astype(F32)
            mixed_b[:, cols] = (gate * jax.nn.sigmoid(gate) * memory[tokens:]).astype(BF16)

    found = contract(
        scores[...], wide_list[...].astype(F32), ((1,), (0,)), precision=lax.Precision.HIGHEST
    )
    grad_weights[...] = jnp.take_along_axis(found, slots[0], axis=1)

    @pl.loop(0, part // CHUNK)
    def _(c):
        cols = pl.ds(pl.multiple_of(c * CHUNK, CHUNK), CHUNK)
        grad_table[:, cols] = summed(z, cols)

    for way in range(2):

        @pl.when((z > 0) if way == 0 else (z < last))
        def _():
            drain(rs_in.at[way, last - 1], rs_recv.at[way, last - 1])
            grad_table[...] += rs_in[way, last - 1].astype(F32)

    drain(asked.at[pl.ds(0, group - 1)], ask_send)
    drain(arrived.at[:, pl.ds(0, group - 1)], grad_send)
    drain(rows_out.at[:, pl.ds(0, plane - 1)], row_send)

    @pl.when(ahead_ok)
    def _():
        drain(col.at[z], tab_send)

    for h in range(1, LAYERS):
        behind = z - step_z * h

        @pl.when((behind >= 0) & (behind <= last))
        def _():
            drain(col.at[behind], par_send)

            @pl.when(ahead_ok)
            def _():
                drain(col.at[behind], tab_send)

    for k in range(last):
        for way in range(2):

            @pl.when(k >= (z if way == 0 else last - z))
            def _():
                drain(rs_out.at[way, k], rs_send)


def asked_width(group):
    return -(-group * ROW_LIMIT // 128) * 128


def local(gate_a, cotangent_a, gate_b, table, row_ids, slots, weights):
    owners = lax.axis_size("table")
    sections = lax.axis_size("section")
    plane = owners // LAYERS
    group = sections * plane
    rows_dev, features = table.shape
    tokens = gate_a.shape[1]
    listed = row_ids.shape[-1]
    picks = slots.shape[-1]
    part = features // sections
    lanes = -(-plane * 2 * ROW_LIMIT // 128) * 128 + asked_width(group)
    slot_rows = owners * 2 * ROW_LIMIT
    vmem = pl.BlockSpec(memory_space=pltpu.VMEM)
    hbm = pl.BlockSpec(memory_space=pl.ANY)
    dma = pltpu.SemaphoreType.DMA
    mixed_b, grad_gate, grad_weights, grad_table = pl.pallas_call(
        exchange,
        out_shape=(
            pltpu.VMEM((tokens, features), BF16),
            pltpu.VMEM((tokens, features), BF16),
            pltpu.VMEM((tokens, picks), F32),
            pltpu.VMEM((rows_dev, part), F32),
        ),
        in_specs=[hbm] * 4 + [vmem] * 3,
        out_specs=(vmem,) * 4,
        scratch_shapes=[
            pltpu.VMEM((tokens, features), BF16),
            pltpu.VMEM((tokens, features), BF16),
            pltpu.VMEM((tokens, features), BF16),
            pltpu.VMEM((LAYERS, rows_dev, features), BF16),
            pltpu.VMEM((picks, 2 * tokens), F32),
            pltpu.VMEM((picks, 2 * tokens), F32),
            pltpu.VMEM((2 * tokens, slot_rows), BF16),
            pltpu.VMEM((owners * ROW_LIMIT, tokens), BF16),
            pltpu.VMEM((slot_rows, listed), BF16),
            pltpu.VMEM((plane, LAYERS, lanes), F32),
            pltpu.VMEM((group, LAYERS, lanes), F32),
            pltpu.VMEM((LAYERS, 1, lanes), F32),
            pltpu.VMEM((sections, plane, LAYERS, ROW_LIMIT, part), BF16),
            pltpu.VMEM((LAYERS, group, ROW_LIMIT, part), BF16),
            pltpu.VMEM((LAYERS, plane, 2 * ROW_LIMIT, features), BF16),
            pltpu.VMEM((plane, LAYERS, 2 * ROW_LIMIT, features), BF16),
            pltpu.VMEM((tokens, features), BF16),
            pltpu.VMEM((tokens, slot_rows), F32),
            pltpu.VMEM((2, LAYERS - 1, rows_dev, part), BF16),
            pltpu.VMEM((2, LAYERS - 1, rows_dev, part), BF16),
            dma((4,)),
            dma, dma,
            dma, dma((LAYERS,)),
            dma, dma((LAYERS,)),
            dma, dma,
            dma, dma((PIECES,)),
            dma, dma((2, LAYERS - 1)),
        ],
        compiler_params=pltpu.CompilerParams(
            collective_id=0, has_side_effects=True, vmem_limit_bytes=60 * 1024 * 1024
        ),
    )(
        gate_a[0], cotangent_a[0], gate_b[0], table, row_ids[0, :, 0], slots[0], weights[0]
    )
    return mixed_b[None], grad_gate[None], grad_weights[None], grad_table


def solution(mesh):
    return jax.shard_map(
        local,
        mesh=mesh,
        in_specs=(
            P("section", "table", None),
            P("section", "table", None),
            P("section", "table", None),
            P("table", None),
            P("section", None, "table", None),
            P("section", None, "table", None),
            P("section", None, "table", None),
        ),
        out_specs=(
            P("section", "table", None),
            P("section", "table", None),
            P("section", "table", None),
            P("table", "section"),
        ),
        check_vma=False,
    )
```

time: 81.1 us -> 47.9 us (0.59)
  the two profiles are of different devices: /device:TPU:7 before, /device:TPU:0 now
where the time goes in v1:
time: 47.9 us; the launch traced here: 47.7 us
  Pallas kernels  44.1 us (92%)
  local copies, waits for them, and re-layouts  3 us (6%)
  between operations  0.64 us (1%)
    pallas_call x1, Pallas kernels, local(): pl.pallas_call(exchange, out_shape=(pltpu.VMEM((tokens, features), BF16),...  44.1 us
    unnamed x4, local copies, waits for them, and re-layouts  3 us

profile of v1, /device:TPU:0, one launch (start us, length us, event | category | flops | bytes accessed | tf_op | source)
XLA Modules:
  0.0 47.7 jit_solution(16299637188000192796)
XLA Ops:
  0.6 44.1 %shard_map.102 = (bf16[64,4096]{1,0:T(8,128)(2,1)S(1)}, bf16[64,4096]{1,0:T(8,128)(2,1)S(1)}, f32[64,128]{1,0:T(8,128)S(1)}, f32[64,2048]{1,0:T(8,128)S(1)}) custom-call(bf16[64,4096]{1,0:T(8,128)(2,1)} %bitcast.12, bf16[64,4096]{1,0:T(8,128)(2,1)} %bitcast.13, bf16[64,4096]{1,0:T(8,128)(2,1)} %bitcast.14, bf16[64,4096]{1,0:T(8,128)(2,1)} %table_in.1, ...), custom_call_target="tpu_custom_call" | custom-call | tf_op jit(solution)/shard_map/pallas_call | solution.py:399
  44.7 0.8 %copy.15 = bf16[1,64,4096]{2,1,0:T(8,128)(2,1)} copy(bf16[1,64,4096]{2,1,0:T(8,128)(2,1)S(1)} %bitcast.10) | data formatting | bytes 1048576
  45.5 0.8 %copy.16 = bf16[1,64,4096]{2,1,0:T(8,128)(2,1)} copy(bf16[1,64,4096]{2,1,0:T(8,128)(2,1)S(1)} %bitcast.9) | data formatting | bytes 1048576
  46.3 0.6 %copy.17 = f32[1,64,128]{2,1,0:T(8,128)} copy(f32[1,64,128]{2,1,0:T(8,128)S(1)} %bitcast.11) | data formatting | bytes 65536
  46.9 0.8 %copy.18 = f32[64,2048]{1,0:T(8,128)} copy(f32[64,2048]{1,0:T(8,128)S(1)} %get-tuple-element.15) | data formatting | bytes 1048576

commit v2 on v1

--- a/solution.py
+++ b/solution.py
@@ -107,6 +107,9 @@
     def other_section(hop):
         return lax.rem(sec + hop, sections)
 
+    def need(k):
+        return jnp.where(z < LAYERS // 2, last - k, k)
+
     def at(layer, place):
         return layer * plane + place
 
@@ -151,6 +154,16 @@
     for q in range(plane):
         message[q] = asking[q * LAYERS : (q + 1) * LAYERS]
 
+    slots_t[...] = jnp.transpose(slots[...].reshape(2 * tokens, -1).astype(F32))
+    weights_t[...] = jnp.transpose(weights[...].reshape(2 * tokens, -1))
+    mixing_t = mix_picks(slots_t, weights_t, listed).astype(BF16)
+    space = iota((owners * 2 * ROW_LIMIT, listed), 0)
+    wide_a = hot(space == spot_a * (2 * ROW_LIMIT) + rank_a)
+    wide_b = hot(space == spot_b * (2 * ROW_LIMIT) + (rank_b + ROW_LIMIT))
+    tall_a = hot(iota((owners * ROW_LIMIT, listed), 0) == spot_a * ROW_LIMIT + rank_a)
+    wide_list[...] = wide_a
+    mix_tall[...] = contract(tall_a, mixing_t[:, :tokens], ((1,), (0,))).astype(BF16)
+
     signals = group - 1 + jnp.where(z > 0, 1, 0) + jnp.where(z < last, 1, 0)
     pl.semaphore_wait(pltpu.get_barrier_semaphore(), signals)
 
@@ -158,7 +171,9 @@
 
     @pl.when(ahead_ok)
     def _():
-        remote(col.at[z], col.at[z], tab_send, tab_recv.at[z], sec, at(z + step_z, p_me))
+        for c in range(PIECES):
+            block = col.at[z, :, pl.ds(c * piece, piece)]
+            remote(block, block, tab_send, tab_recv.at[z, c], sec, at(z + step_z, p_me))
 
     for hop in range(plane):
         q = peer(hop)
@@ -170,16 +185,6 @@
                 )
     pltpu.make_async_copy(message.at[p_me], asked.at[seat], ask_recv).start()
 
-    slots_t[...] = jnp.transpose(slots[...].reshape(2 * tokens, -1).astype(F32))
-    weights_t[...] = jnp.transpose(weights[...].reshape(2 * tokens, -1))
-    mixing_t = mix_picks(slots_t, weights_t, listed).astype(BF16)
-    space = iota((owners * 2 * ROW_LIMIT, listed), 0)
-    wide_a = hot(space == spot_a * (2 * ROW_LIMIT) + rank_a)
-    wide_b = hot(space == spot_b * (2 * ROW_LIMIT) + (rank_b + ROW_LIMIT))
-    tall_a = hot(iota((owners * ROW_LIMIT, listed), 0) == spot_a * ROW_LIMIT + rank_a)
-    wide_list[...] = wide_a
-    mix_tall[...] = contract(tall_a, mixing_t[:, :tokens], ((1,), (0,))).astype(BF16)
-
     drain(gate_a, load.at[1])
     drain(cot_a, load.at[2])
     for half in range(sections):
@@ -194,23 +199,27 @@
             rows = contract(mix_tall[...], value, ((1,), (0,))).astype(BF16)
             grads_out[half, :, :, :, inner] = rows.reshape(plane, LAYERS, ROW_LIMIT, CHUNK)
 
-        for hop in range(1, plane):
-            q = peer(hop)
-            remote(
-                grads_out.at[half, q], arrived.at[:, seat], grad_send, grad_recv, half, at(z, q)
-            )
-
-        @pl.when(sec == half)
-        def _():
-            pltpu.make_async_copy(
-                grads_out.at[half, p_me], arrived.at[:, seat], grad_recv
-            ).start()
-
-        @pl.when(sec != half)
-        def _():
-            remote(
-                grads_out.at[half, p_me], arrived.at[:, seat], grad_send, grad_recv, half, me
-            )
+        for k in range(LAYERS):
+            layer = need(k)
+            for hop in range(1, plane):
+                q = peer(hop)
+                remote(
+                    grads_out.at[half, q, layer], arrived.at[layer, seat],
+                    grad_send, grad_recv.at[layer], half, at(z, q),
+                )
+
+            @pl.when(sec == half)
+            def _():
+                pltpu.make_async_copy(
+                    grads_out.at[half, p_me, layer], arrived.at[layer, seat], grad_recv.at[layer]
+                ).start()
+
+            @pl.when(sec != half)
+            def _():
+                remote(
+                    grads_out.at[half, p_me, layer], arrived.at[layer, seat],
+                    grad_send, grad_recv.at[layer], half, me,
+                )
 
     drain(asked, ask_recv)
     serving, summing = asked[sec * plane, :, :width], asked[0, :, width:]
@@ -222,26 +231,26 @@
         codes[layer, :, :width] = serving[layer : layer + 1]
         codes[layer, :, width:] = summing[layer : layer + 1]
 
-    def serve(layer):
+    def lookup(layer):
         code = codes[layer, :, :width]
         pick = (iota((rows_dev, width), 0).astype(F32) == code - 1.0).astype(F32)
-        pick = jnp.transpose(pick)[: plane * 2 * ROW_LIMIT].astype(BF16)
-        for c in range(PIECES):
-            for k in range(piece // CHUNK):
-                cols = pl.ds(c * piece + k * CHUNK, CHUNK)
-                rows = contract(pick, col[layer, :, cols], ((1,), (0,))).astype(BF16)
-                rows_out[layer, :, :, cols] = rows.reshape(plane, 2 * ROW_LIMIT, CHUNK)
-            cols = pl.ds(c * piece, piece)
-            for hop in range(1, plane):
-                q = peer(hop)
-                remote(
-                    rows_out.at[layer, q, :, cols], fetched.at[p_me, layer, :, cols],
-                    row_send, row_recv.at[c], sec, at(z, q),
-                )
-            pltpu.make_async_copy(
-                rows_out.at[layer, p_me, :, cols], fetched.at[p_me, layer, :, cols],
-                row_recv.at[c],
-            ).start()
+        return jnp.transpose(pick)[: plane * 2 * ROW_LIMIT].astype(BF16)
+
+    def serve(layer, pick, c):
+        for k in range(piece // CHUNK):
+            cols = pl.ds(c * piece + k * CHUNK, CHUNK)
+            rows = contract(pick, col[layer, :, cols], ((1,), (0,))).astype(BF16)
+            rows_out[layer, :, :, cols] = rows.reshape(plane, 2 * ROW_LIMIT, CHUNK)
+        cols = pl.ds(c * piece, piece)
+        for hop in range(1, plane):
+            q = peer(hop)
+            remote(
+                rows_out.at[layer, q, :, cols], fetched.at[p_me, layer, :, cols],
+                row_send, row_recv.at[c], sec, at(z, q),
+            )
+        pltpu.make_async_copy(
+            rows_out.at[layer, p_me, :, cols], fetched.at[p_me, layer, :, cols], row_recv.at[c]
+        ).start()
 
     def summed(layer, cols):
         code = codes[layer, :, width:][:, : group * ROW_LIMIT]
@@ -254,22 +263,27 @@
 
         @pl.when((behind >= 0) & (behind <= last))
         def _():
-            drain(col.at[behind], tab_recv.at[behind])
-
-            @pl.when(ahead_ok)
-            def _():
-                remote(
-                    col.at[behind], col.at[behind], tab_send, tab_recv.at[behind],
-                    sec, at(z + step_z, p_me),
-                )
-
-            remote(col.at[behind], col.at[behind], par_send, par_recv.at[behind], partner, me)
-            serve(behind)
+            pick = lookup(behind)
+            for c in range(PIECES):
+                block = col.at[behind, :, pl.ds(c * piece, piece)]
+                drain(block, tab_recv.at[behind, c])
+
+                @pl.when(ahead_ok)
+                def _():
+                    remote(
+                        block, block, tab_send, tab_recv.at[behind, c],
+                        sec, at(z + step_z, p_me),
+                    )
+
+                remote(block, block, par_send, par_recv.at[behind, c], partner, me)
+                serve(behind, pick, c)
 
         @pl.when((ahead >= 0) & (ahead <= last))
         def _():
-            drain(col.at[ahead], par_recv.at[ahead])
-            serve(ahead)
+            pick = lookup(ahead)
+            for c in range(PIECES):
+                drain(col.at[ahead, :, pl.ds(c * piece, piece)], par_recv.at[ahead, c])
+                serve(ahead, pick, c)
 
     def reduce_step(k):
         for way in range(2):
@@ -279,18 +293,22 @@
             target = z + 1 if way == 0 else z - 1
 
             def pass_on(earlier):
-                @pl.loop(0, part // CHUNK)
-                def _(c):
-                    cols = pl.ds(pl.multiple_of(c * CHUNK, CHUNK), CHUNK)
+                for c in range(2):
+                    cols = pl.ds(c * (part // 2), part // 2)
+                    if earlier:
+                        drain(rs_in.at[way, k - 1, :, cols], rs_recv.at[way, k - 1, c])
                     total = summed(layer, cols)
                     if earlier:
                         total = total + rs_in[way, k - 1, :, cols].astype(F32)
                     rs_out[way, k, :, cols] = total.astype(BF16)
-
-                remote(
-                    rs_out.at[way, k], rs_in.at[way, k], rs_send, rs_recv.at[way, k],
-                    sec, at(target, p_me),
-                )
+                    remote(
+                        rs_out.at[way, k, :, cols], rs_in.at[way, k, :, cols],
+                        rs_send, rs_recv.at[way, k, c], sec, at(target, p_me),
+                    )
+
+            @pl.when(place <= k)
+            def _():
+                drain(arrived.at[layer], grad_recv.at[layer])
 
             @pl.when(place == 0)
             def _():
@@ -300,21 +318,28 @@
 
                 @pl.when((place > 0) & (place <= k))
                 def _():
-                    drain(rs_in.at[way, k - 1], rs_recv.at[way, k - 1])
                     pass_on(True)
 
-    serve(z)
+    pick = lookup(z)
+    for c in range(PIECES):
+        serve(z, pick, c)
+    reduce_step(0)
     table_hop(1)
 
     mix_wide[:tokens] = contract(mixing_t[:, :tokens], wide_a, ((0,), (1,))).astype(BF16)
     mix_wide[tokens:] = contract(mixing_t[:, tokens:], wide_b, ((0,), (1,))).astype(BF16)
     scores[...] = jnp.zeros_like(scores)
-    drain(arrived, grad_recv)
 
     for h in range(2, LAYERS):
-        reduce_step(h - 2)
         table_hop(h)
-    reduce_step(LAYERS - 2)
+        reduce_step(h - 1)
+
+    drain(arrived.at[z], grad_recv.at[z])
+
+    @pl.loop(0, part // CHUNK)
+    def _(c):
+        cols = pl.ds(pl.multiple_of(c * CHUNK, CHUNK), CHUNK)
+        grad_table[:, cols] = summed(z, cols)
 
     drain(gate_b, load.at[3])
     for c in range(PIECES):
@@ -338,17 +363,14 @@
     )
     grad_weights[...] = jnp.take_along_axis(found, slots[0], axis=1)
 
-    @pl.loop(0, part // CHUNK)
-    def _(c):
-        cols = pl.ds(pl.multiple_of(c * CHUNK, CHUNK), CHUNK)
-        grad_table[:, cols] = summed(z, cols)
-
     for way in range(2):
 
         @pl.when((z > 0) if way == 0 else (z < last))
         def _():
-            drain(rs_in.at[way, last - 1], rs_recv.at[way, last - 1])
-            grad_table[...] += rs_in[way, last - 1].astype(F32)
+            for c in range(2):
+                cols = pl.ds(c * (part // 2), part // 2)
+                drain(rs_in.at[way, last - 1, :, cols], rs_recv.at[way, last - 1, c])
+                grad_table[:, cols] += rs_in[way, last - 1, :, cols].astype(F32)
 
     drain(asked.at[pl.ds(0, group - 1)], ask_send)
     drain(arrived.at[:, pl.ds(0, group - 1)], grad_send)
@@ -375,6 +397,18 @@
             @pl.when(k >= (z if way == 0 else last - z))
             def _():
                 drain(rs_out.at[way, k], rs_send)
+
+
+def store(mixed_b, grad_gate, grad_weights, grad_table, *refs):
+    outs, sems = refs[:4], refs[4]
+    copies = [
+        pltpu.make_async_copy(source, target, sems.at[n])
+        for n, (source, target) in enumerate(zip((mixed_b, grad_gate, grad_weights, grad_table), outs))
+    ]
+    for copy in copies:
+        copy.start()
+    for copy in copies:
+        copy.wait()
 
 
 def asked_width(group):
@@ -429,11 +463,11 @@
             pltpu.VMEM((2, LAYERS - 1, rows_dev, part), BF16),
             dma((4,)),
             dma, dma,
+            dma, dma((LAYERS, PIECES)),
+            dma, dma((LAYERS, PIECES)),
             dma, dma((LAYERS,)),
-            dma, dma((LAYERS,)),
-            dma, dma,
             dma, dma((PIECES,)),
-            dma, dma((2, LAYERS - 1)),
+            dma, dma((2, LAYERS - 1, 2)),
         ],
         compiler_params=pltpu.CompilerParams(
             collective_id=0, has_side_effects=True, vmem_limit_bytes=60 * 1024 * 1024
@@ -441,6 +475,14 @@
     )(
         gate_a[0], cotangent_a[0], gate_b[0], table, row_ids[0, :, 0], slots[0], weights[0]
     )
+    results = (mixed_b, grad_gate, grad_weights, grad_table)
+    mixed_b, grad_gate, grad_weights, grad_table = pl.pallas_call(
+        store,
+        out_shape=tuple(jax.ShapeDtypeStruct(r.shape, r.dtype) for r in results),
+        in_specs=[vmem] * 4,
+        out_specs=(hbm,) * 4,
+        scratch_shapes=[dma((4,))],
+    )(*(pltpu.with_memory_space_constraint(r, pltpu.VMEM) for r in results))
     return mixed_b[None], grad_gate[None], grad_weights[None], grad_table
 
 

time: 47.9 us -> 45 us (0.939)
  local copies, waits for them, and re-layouts: 3 us -> 0 us
    unnamed x4 -> x0, local copies, waits for them, and re-layouts: 3 us -> none
    pallas_call x0 -> x1, Pallas kernels: none -> 1.19 us  [local(): pl.pallas_call(store, out_shape=tuple((jax.ShapeDtypeStruct(r.shape, r.dt...]
    pallas_call x1, Pallas kernels: 44.1 us -> 43 us  [local(): pl.pallas_call(exchange, out_shape=(pltpu.VMEM((tokens, features), BF16),...]
where the time goes in v2:
time: 45 us; the launch traced here: 44.8 us
  Pallas kernels  44.2 us (98%)
  between operations  0.64 us (1%)
    pallas_call x1, Pallas kernels, local(): pl.pallas_call(exchange, out_shape=(pltpu.VMEM((tokens, features), BF16),...  43 us
    pallas_call x1, Pallas kernels, local(): pl.pallas_call(store, out_shape=tuple((jax.ShapeDtypeStruct(r.shape, r.dt...  1.19 us

profile of v2, /device:TPU:0, one launch (start us, length us, event | category | flops | bytes accessed | tf_op | source)
XLA Modules:
  0.0 44.8 jit_solution(10226224393725108873)
XLA Ops:
  0.6 43.0 %shard_map.102 = (bf16[64,4096]{1,0:T(8,128)(2,1)S(1)}, bf16[64,4096]{1,0:T(8,128)(2,1)S(1)}, f32[64,128]{1,0:T(8,128)S(1)}, f32[64,2048]{1,0:T(8,128)S(1)}) custom-call(bf16[64,4096]{1,0:T(8,128)(2,1)} %bitcast.9, bf16[64,4096]{1,0:T(8,128)(2,1)} %bitcast.10, bf16[64,4096]{1,0:T(8,128)(2,1)} %bitcast.11, bf16[64,4096]{1,0:T(8,128)(2,1)} %table_in.1, ...), custom_call_target="tpu_custom_call" | custom-call | tf_op jit(solution)/shard_map/pallas_call | solution.py:433
  43.6 1.2 %shard_map.103 = (bf16[64,4096]{1,0:T(8,128)(2,1)}, bf16[64,4096]{1,0:T(8,128)(2,1)}, f32[64,128]{1,0:T(8,128)}, f32[64,2048]{1,0:T(8,128)}) custom-call(bf16[64,4096]{1,0:T(8,128)(2,1)S(1)} %get-tuple-element.12.mixed_b, bf16[64,4096]{1,0:T(8,128)(2,1)S(1)} %get-tuple-element.13.grad_gate, f32[64,128]{1,0:T(8,128)S(1)} %get-tuple-element.14.grad_weights, ...), custom_call_target="tpu_custom_call" | custom-call | tf_op jit(solution)/shard_map/pallas_call | solution.py:479

commit v3 on v2

--- a/solution.py
+++ b/solution.py
@@ -66,10 +66,11 @@
 def exchange(
     gate_a_in, cot_a_in, gate_b_in, table_in, row_ids, slots, weights,
     mixed_b, grad_gate, grad_weights, grad_table,
-    gate_a, cot_a, gate_b, col, slots_t, weights_t, mix_wide, mix_tall, wide_list,
-    message, asked, codes, grads_out, arrived, rows_out, fetched, grad_memory, scores,
+    gate_a, cot_a, gate_b, col, aux, slots_t, weights_t, mix_wide, mix_tall, wide_list,
+    message, asked, asked_far, codes, codes_aux, grads_out, arrived, rows_out, rows_aux, fetched,
+    grad_memory, scores,
     rs_out, rs_in,
-    load, ask_send, ask_recv, tab_send, tab_recv, par_send, par_recv,
+    load, ask_send, ask_recv, far_recv, tab_send, tab_recv, par_send, par_recv, aux_recv,
     grad_send, grad_recv, row_send, row_recv, rs_send, rs_recv,
 ):
     sections = lax.axis_size("section")
@@ -95,14 +96,19 @@
     ahead_ok = (z + step_z >= 0) & (z + step_z <= last)
 
     def peer(hop):
-        if plane & (plane - 1):
-            return lax.rem(p_me + hop, plane)
         other, bit = p_me, 1
         while bit < plane:
             if hop & bit:
                 other = other + bit - 2 * bit * lax.rem(p_me // bit, 2)
             bit *= 2
         return other
+
+    x_side, y_side, corner = peer(1), peer(2), peer(3)
+
+    def strip(c):
+        if isinstance(c, int):
+            return pl.ds(c * piece, piece)
+        return pl.ds(pl.multiple_of(c * piece, piece), piece)
 
     def other_section(hop):
         return lax.rem(sec + hop, sections)
@@ -175,6 +181,16 @@
             block = col.at[z, :, pl.ds(c * piece, piece)]
             remote(block, block, tab_send, tab_recv.at[z, c], sec, at(z + step_z, p_me))
 
+    for j, side in enumerate((x_side, y_side)):
+        cols = strip(2 * j + parity)
+        remote(
+            col.at[z, :, cols], aux.at[z, :, cols], tab_send, aux_recv.at[z, 2 * j + parity],
+            sec, at(z, side),
+        )
+        remote(
+            message.at[corner], asked_far.at[1 - j], ask_send, far_recv, sec, at(z, side)
+        )
+
     for hop in range(plane):
         q = peer(hop)
         for turn in range(sections):
@@ -231,26 +247,50 @@
         codes[layer, :, :width] = serving[layer : layer + 1]
         codes[layer, :, width:] = summing[layer : layer + 1]
 
-    def lookup(layer):
-        code = codes[layer, :, :width]
+    drain(asked_far, far_recv)
+    for j, side in enumerate((x_side, y_side)):
+        serving = message[side, :, :width] + asked_far[j, :, :width]
+        for layer in range(LAYERS):
+            codes_aux[j, layer] = serving[layer : layer + 1]
+
+    def lookup(code):
         pick = (iota((rows_dev, width), 0).astype(F32) == code - 1.0).astype(F32)
         return jnp.transpose(pick)[: plane * 2 * ROW_LIMIT].astype(BF16)
 
-    def serve(layer, pick, c):
+    def look_aside(layer):
+        return [lookup(codes_aux[j, layer]) for j in range(2)]
+
+    def find(pick, held, found, layer, c):
         for k in range(piece // CHUNK):
             cols = pl.ds(c * piece + k * CHUNK, CHUNK)
-            rows = contract(pick, col[layer, :, cols], ((1,), (0,))).astype(BF16)
-            rows_out[layer, :, :, cols] = rows.reshape(plane, 2 * ROW_LIMIT, CHUNK)
-        cols = pl.ds(c * piece, piece)
-        for hop in range(1, plane):
-            q = peer(hop)
-            remote(
-                rows_out.at[layer, q, :, cols], fetched.at[p_me, layer, :, cols],
-                row_send, row_recv.at[c], sec, at(z, q),
-            )
+            rows = contract(pick, held[layer, :, cols], ((1,), (0,))).astype(BF16)
+            found[layer, :, :, cols] = rows.reshape(plane, 2 * ROW_LIMIT, CHUNK)
+
+    def give(found, layer, c, q, column):
+        remote(
+            found.at[layer, q, :, strip(c)], fetched.at[column, layer, :, strip(c)],
+            row_send, row_recv.at[c], sec, at(z, q),
+        )
+
+    def keep(found, layer, c, column):
         pltpu.make_async_copy(
-            rows_out.at[layer, p_me, :, cols], fetched.at[p_me, layer, :, cols], row_recv.at[c]
+            found.at[layer, p_me, :, strip(c)], fetched.at[column, layer, :, strip(c)],
+            row_recv.at[c],
         ).start()
+
+    def serve(layer, pick, c, shared):
+        find(pick, col, rows_out, layer, c)
+        hops = [2 if c < PIECES // 2 else 1, *range(4, plane)] if shared else range(1, plane)
+        for hop in hops:
+            give(rows_out, layer, c, peer(hop), p_me)
+        keep(rows_out, layer, c, p_me)
+
+    def serve_aside(layer, picks, c):
+        j = 2 * c // PIECES
+        column, target = ((x_side, y_side), (y_side, x_side))[j]
+        find(picks[j], aux, rows_aux, layer, c)
+        give(rows_aux, layer, c, target, column)
+        keep(rows_aux, layer, c, column)
 
     def summed(layer, cols):
         code = codes[layer, :, width:][:, : group * ROW_LIMIT]
@@ -263,7 +303,7 @@
 
         @pl.when((behind >= 0) & (behind <= last))
         def _():
-            pick = lookup(behind)
+            pick = lookup(codes[behind, :, :width])
             for c in range(PIECES):
                 block = col.at[behind, :, pl.ds(c * piece, piece)]
                 drain(block, tab_recv.at[behind, c])
@@ -276,14 +316,40 @@
                     )
 
                 remote(block, block, par_send, par_recv.at[behind, c], partner, me)
-                serve(behind, pick, c)
+                serve(behind, pick, c, h == 1)
 
         @pl.when((ahead >= 0) & (ahead <= last))
         def _():
-            pick = lookup(ahead)
+            pick = lookup(codes[ahead, :, :width])
             for c in range(PIECES):
                 drain(col.at[ahead, :, pl.ds(c * piece, piece)], par_recv.at[ahead, c])
-                serve(ahead, pick, c)
+                serve(ahead, pick, c, h == 1)
+
+    def own_aside():
+        for j in range(2):
+            c = 2 * j + parity
+            block = aux.at[z, :, strip(c)]
+            drain(block, aux_recv.at[z, c])
+            remote(block, block, par_send, aux_recv.at[z, c], partner, me)
+
+    def near_aside():
+        behind, ahead = z - step_z, z + step_z
+
+        @pl.when((behind >= 0) & (behind <= last))
+        def _():
+            picks = look_aside(behind)
+            for c in range(PIECES):
+                block = aux.at[behind, :, strip(c)]
+                drain(block, aux_recv.at[behind, c])
+                remote(block, block, par_send, aux_recv.at[behind, c], partner, me)
+                serve_aside(behind, picks, c)
+
+        @pl.when(ahead_ok)
+        def _():
+            picks = look_aside(ahead)
+            for c in range(PIECES):
+                drain(aux.at[ahead, :, strip(c)], aux_recv.at[ahead, c])
+                serve_aside(ahead, picks, c)
 
     def reduce_step(k):
         for way in range(2):
@@ -320,11 +386,24 @@
                 def _():
                     pass_on(True)
 
-    pick = lookup(z)
+    own_aside()
+    pick = lookup(codes[z, :, :width])
     for c in range(PIECES):
-        serve(z, pick, c)
+        serve(z, pick, c, True)
+    for j in range(2):
+        c = 2 * j + 1 - parity
+        drain(aux.at[z, :, strip(c)], aux_recv.at[z, c])
+    picks = look_aside(z)
+    for c in range(PIECES):
+        serve_aside(z, picks, c)
     reduce_step(0)
     table_hop(1)
+
+    @pl.when(ahead_ok)
+    def _():
+        for c in range(PIECES):
+            block = aux.at[z, :, strip(c)]
+            remote(block, block, tab_send, aux_recv.at[z, c], sec, at(z + step_z, p_me))
 
     mix_wide[:tokens] = contract(mixing_t[:, :tokens], wide_a, ((0,), (1,))).astype(BF16)
     mix_wide[tokens:] = contract(mixing_t[:, tokens:], wide_b, ((0,), (1,))).astype(BF16)
@@ -333,6 +412,8 @@
     for h in range(2, LAYERS):
         table_hop(h)
         reduce_step(h - 1)
+        if h == 2:
+            near_aside()
 
     drain(arrived.at[z], grad_recv.at[z])
 
@@ -374,22 +455,34 @@
 
     drain(asked.at[pl.ds(0, group - 1)], ask_send)
     drain(arrived.at[:, pl.ds(0, group - 1)], grad_send)
-    drain(rows_out.at[:, pl.ds(0, plane - 1)], row_send)
+    drain(asked_far, ask_send)
+    drain(rows_out.at[0, pl.ds(0, plane - 2)], row_send)
+    for c in range(2):
+        drain(col.at[z, :, strip(c)], tab_send)
+        drain(col.at[z, :, strip(c)], par_send)
 
     @pl.when(ahead_ok)
     def _():
         drain(col.at[z], tab_send)
+        drain(col.at[z], tab_send)
 
     for h in range(1, LAYERS):
-        behind = z - step_z * h
+        behind, ahead = z - step_z * h, z + step_z * h
 
         @pl.when((behind >= 0) & (behind <= last))
         def _():
+            drain(rows_out.at[0, pl.ds(0, plane - (2 if h == 1 else 1))], row_send)
             drain(col.at[behind], par_send)
+            if h == 1:
+                drain(col.at[behind], par_send)
 
             @pl.when(ahead_ok)
             def _():
                 drain(col.at[behind], tab_send)
+
+        @pl.when((ahead >= 0) & (ahead <= last))
+        def _():
+            drain(rows_out.at[0, pl.ds(0, plane - (2 if h == 1 else 1))], row_send)
 
     for k in range(last):
         for way in range(2):
@@ -445,6 +538,7 @@
             pltpu.VMEM((tokens, features), BF16),
             pltpu.VMEM((tokens, features), BF16),
             pltpu.VMEM((LAYERS, rows_dev, features), BF16),
+            pltpu.VMEM((LAYERS, rows_dev, features), BF16),
             pltpu.VMEM((picks, 2 * tokens), F32),
             pltpu.VMEM((picks, 2 * tokens), F32),
             pltpu.VMEM((2 * tokens, slot_rows), BF16),
@@ -452,9 +546,12 @@
             pltpu.VMEM((slot_rows, listed), BF16),
             pltpu.VMEM((plane, LAYERS, lanes), F32),
             pltpu.VMEM((group, LAYERS, lanes), F32),
+            pltpu.VMEM((2, LAYERS, lanes), F32),
             pltpu.VMEM((LAYERS, 1, lanes), F32),
+            pltpu.VMEM((2, LAYERS, 1, lanes - asked_width(group)), F32),
             pltpu.VMEM((sections, plane, LAYERS, ROW_LIMIT, part), BF16),
             pltpu.VMEM((LAYERS, group, ROW_LIMIT, part), BF16),
+            pltpu.VMEM((LAYERS, plane, 2 * ROW_LIMIT, features), BF16),
             pltpu.VMEM((LAYERS, plane, 2 * ROW_LIMIT, features), BF16),
             pltpu.VMEM((plane, LAYERS, 2 * ROW_LIMIT, features), BF16),
             pltpu.VMEM((tokens, features), BF16),
@@ -462,9 +559,9 @@
             pltpu.VMEM((2, LAYERS - 1, rows_dev, part), BF16),
             pltpu.VMEM((2, LAYERS - 1, rows_dev, part), BF16),
             dma((4,)),
-            dma, dma,
+            dma, dma, dma,
             dma, dma((LAYERS, PIECES)),
-            dma, dma((LAYERS, PIECES)),
+            dma, dma((LAYERS, PIECES)), dma((LAYERS, PIECES)),
             dma, dma((LAYERS,)),
             dma, dma((PIECES,)),
             dma, dma((2, LAYERS - 1, 2)),

time: 45 us -> 43.6 us (0.969)
  Pallas kernels: 44.2 us -> 42.8 us
    pallas_call x1, Pallas kernels: 43 us -> 41.6 us  [local(): pl.pallas_call(exchange, out_shape=(pltpu.VMEM((tokens, features), BF16),...]
where the time goes in v3:
time: 43.6 us; the launch traced here: 43.5 us
  Pallas kernels  42.8 us (98%)
  between operations  0.64 us (1%)
    pallas_call x1, Pallas kernels, local(): pl.pallas_call(exchange, out_shape=(pltpu.VMEM((tokens, features), BF16),...  41.6 us
    pallas_call x1, Pallas kernels, local(): pl.pallas_call(store, out_shape=tuple((jax.ShapeDtypeStruct(r.shape, r.dt...  1.19 us

profile of v3, /device:TPU:0, one launch (start us, length us, event | category | flops | bytes accessed | tf_op | source)
XLA Modules:
  0.0 43.5 jit_solution(8093983243960829185)
XLA Ops:
  0.6 41.6 %shard_map.102 = (bf16[64,4096]{1,0:T(8,128)(2,1)S(1)}, bf16[64,4096]{1,0:T(8,128)(2,1)S(1)}, f32[64,128]{1,0:T(8,128)S(1)}, f32[64,2048]{1,0:T(8,128)S(1)}) custom-call(bf16[64,4096]{1,0:T(8,128)(2,1)} %bitcast.9, bf16[64,4096]{1,0:T(8,128)(2,1)} %bitcast.10, bf16[64,4096]{1,0:T(8,128)(2,1)} %bitcast.11, bf16[64,4096]{1,0:T(8,128)(2,1)} %table_in.1, ...), custom_call_target="tpu_custom_call" | custom-call | tf_op jit(solution)/shard_map/pallas_call | solution.py:526
  42.3 1.2 %shard_map.103 = (bf16[64,4096]{1,0:T(8,128)(2,1)}, bf16[64,4096]{1,0:T(8,128)(2,1)}, f32[64,128]{1,0:T(8,128)}, f32[64,2048]{1,0:T(8,128)}) custom-call(bf16[64,4096]{1,0:T(8,128)(2,1)S(1)} %get-tuple-element.12.mixed_b, bf16[64,4096]{1,0:T(8,128)(2,1)S(1)} %get-tuple-element.13.grad_gate, f32[64,128]{1,0:T(8,128)S(1)} %get-tuple-element.14.grad_weights, ...), custom_call_target="tpu_custom_call" | custom-call | tf_op jit(solution)/shard_map/pallas_call | solution.py:576

commit v4 on v3

--- a/solution.py
+++ b/solution.py
@@ -9,6 +9,7 @@
 CHUNK = 512
 LAYERS = 4
 PIECES = 4
+HALVES = 2
 UNROLL = 8
 MESH = pl.DeviceIdType.MESH
 BF16, F32 = jnp.bfloat16, jnp.float32
@@ -64,14 +65,13 @@
 
 
 def exchange(
-    gate_a_in, cot_a_in, gate_b_in, table_in, row_ids, slots, weights,
+    gate_a_in, cot_a_in, gate_b_in, table_in, row_ids_in, slots_in, weights_in,
     mixed_b, grad_gate, grad_weights, grad_table,
-    gate_a, cot_a, gate_b, col, aux, slots_t, weights_t, mix_wide, mix_tall, wide_list,
-    message, asked, asked_far, codes, codes_aux, grads_out, arrived, rows_out, rows_aux, fetched,
+    gate_a, cot_a, gate_b, row_ids, slots, weights, col, aux, slots_t, weights_t, mix_wide, mix_tall, wide_list,
+    message, asked, codes, codes_sum, codes_aux, grads_out, arrived, rows_out, rows_aux, fetched,
     grad_memory, scores,
     rs_out, rs_in,
-    load, ask_send, ask_recv, far_recv, tab_send, tab_recv, par_send, par_recv, aux_recv,
-    grad_send, grad_recv, row_send, row_recv, rs_send, rs_recv,
+    load, send, ask_recv, tab_recv, par_recv, aux_recv, grad_recv, row_recv, rs_recv,
 ):
     sections = lax.axis_size("section")
     owners = lax.axis_size("table")
@@ -81,7 +81,7 @@
     listed = row_ids.shape[1]
     part = features // sections
     group = sections * plane
-    width = codes.shape[2] - asked_width(group)
+    width = group * ROW_LIMIT
     piece = features // PIECES
     last = LAYERS - 1
 
@@ -110,6 +110,9 @@
             return pl.ds(c * piece, piece)
         return pl.ds(pl.multiple_of(c * piece, piece), piece)
 
+    def half(n):
+        return pl.ds(n * (features // HALVES), features // HALVES)
+
     def other_section(hop):
         return lax.rem(sec + hop, sections)
 
@@ -144,22 +147,60 @@
     def _():
         greet(sec, at(z + 1, p_me))
 
+    pltpu.make_async_copy(row_ids_in, row_ids, load.at[4]).start()
     pltpu.make_async_copy(table_in, col.at[z], load.at[0]).start()
+    pltpu.make_async_copy(slots_in, slots, load.at[5]).start()
+    pltpu.make_async_copy(weights_in, weights, load.at[6]).start()
     pltpu.make_async_copy(gate_a_in, gate_a, load.at[1]).start()
     pltpu.make_async_copy(cot_a_in, cot_a, load.at[2]).start()
     pltpu.make_async_copy(gate_b_in, gate_b, load.at[3]).start()
 
+    drain(row_ids, load.at[4])
     ids = row_ids[...]
     rank_a, spot_a, held_a = locate(ids[0:1], owners, plane, rows_dev)
     rank_b, spot_b, held_b = locate(ids[1:2], owners, plane, rows_dev)
     lane = iota((codes.shape[2], listed), 0)
-    base = p_me * (2 * ROW_LIMIT)
-    lanes_a = hot((lane == rank_a + base) | (lane == rank_a + (seat * ROW_LIMIT + width)))
+    base = p_me * (2 * ROW_LIMIT) + width
+    lanes_a = hot((lane == rank_a + base) | (lane == rank_a + seat * ROW_LIMIT))
     lanes_b = hot(lane == rank_b + (base + ROW_LIMIT))
     asking = contract(held_a, lanes_a, ((1,), (1,))) + contract(held_b, lanes_b, ((1,), (1,)))
     for q in range(plane):
         message[q] = asking[q * LAYERS : (q + 1) * LAYERS]
 
+    signals = group - 1 + jnp.where(z > 0, 1, 0) + jnp.where(z < last, 1, 0)
+    pl.semaphore_wait(pltpu.get_barrier_semaphore(), signals)
+
+    for hop in range(plane):
+        q = peer(hop)
+        for turn in range(sections):
+            if hop or turn:
+                remote(
+                    message.at[q], asked.at[seat], send, ask_recv,
+                    other_section(turn), at(z, q),
+                )
+    pltpu.make_async_copy(message.at[p_me], asked.at[seat], ask_recv).start()
+
+    for j, side in enumerate((x_side, y_side)):
+        remote(
+            message.at[corner], asked.at[group + 1 - j], send, ask_recv, sec, at(z, side)
+        )
+
+    drain(col.at[z], load.at[0])
+
+    @pl.when(ahead_ok)
+    def _():
+        for n in range(HALVES):
+            block = col.at[z, :, half(n)]
+            remote(block, block, send, tab_recv.at[0, n], sec, at(z + step_z, p_me))
+
+    for j, side in enumerate((x_side, y_side)):
+        cols = strip(2 * j + parity)
+        remote(
+            col.at[z, :, cols], aux.at[z, :, cols], send, aux_recv.at[0], sec, at(z, side),
+        )
+
+    drain(slots, load.at[5])
+    drain(weights, load.at[6])
     slots_t[...] = jnp.transpose(slots[...].reshape(2 * tokens, -1).astype(F32))
     weights_t[...] = jnp.transpose(weights[...].reshape(2 * tokens, -1))
     mixing_t = mix_picks(slots_t, weights_t, listed).astype(BF16)
@@ -170,92 +211,53 @@
     wide_list[...] = wide_a
     mix_tall[...] = contract(tall_a, mixing_t[:, :tokens], ((1,), (0,))).astype(BF16)
 
-    signals = group - 1 + jnp.where(z > 0, 1, 0) + jnp.where(z < last, 1, 0)
-    pl.semaphore_wait(pltpu.get_barrier_semaphore(), signals)
-
-    drain(col.at[z], load.at[0])
-
-    @pl.when(ahead_ok)
-    def _():
-        for c in range(PIECES):
-            block = col.at[z, :, pl.ds(c * piece, piece)]
-            remote(block, block, tab_send, tab_recv.at[z, c], sec, at(z + step_z, p_me))
-
-    for j, side in enumerate((x_side, y_side)):
-        cols = strip(2 * j + parity)
-        remote(
-            col.at[z, :, cols], aux.at[z, :, cols], tab_send, aux_recv.at[z, 2 * j + parity],
-            sec, at(z, side),
-        )
-        remote(
-            message.at[corner], asked_far.at[1 - j], ask_send, far_recv, sec, at(z, side)
-        )
-
-    for hop in range(plane):
-        q = peer(hop)
-        for turn in range(sections):
-            if hop or turn:
-                remote(
-                    message.at[q], asked.at[seat], ask_send, ask_recv,
-                    other_section(turn), at(z, q),
-                )
-    pltpu.make_async_copy(message.at[p_me], asked.at[seat], ask_recv).start()
-
     drain(gate_a, load.at[1])
     drain(cot_a, load.at[2])
-    for half in range(sections):
-
-        @pl.loop(0, part // CHUNK)
-        def _(c):
-            inner = pl.ds(pl.multiple_of(c * CHUNK, CHUNK), CHUNK)
-            cols = pl.ds(pl.multiple_of(half * part + c * CHUNK, CHUNK), CHUNK)
-            gate = gate_a[:, cols].astype(F32)
-            value = (cot_a[:, cols].astype(F32) * gate * jax.nn.sigmoid(gate)).astype(BF16)
-            grad_memory[:, cols] = value
-            rows = contract(mix_tall[...], value, ((1,), (0,))).astype(BF16)
-            grads_out[half, :, :, :, inner] = rows.reshape(plane, LAYERS, ROW_LIMIT, CHUNK)
-
-        for k in range(LAYERS):
-            layer = need(k)
-            for hop in range(1, plane):
-                q = peer(hop)
-                remote(
-                    grads_out.at[half, q, layer], arrived.at[layer, seat],
-                    grad_send, grad_recv.at[layer], half, at(z, q),
-                )
-
-            @pl.when(sec == half)
-            def _():
-                pltpu.make_async_copy(
-                    grads_out.at[half, p_me, layer], arrived.at[layer, seat], grad_recv.at[layer]
-                ).start()
-
-            @pl.when(sec != half)
-            def _():
-                remote(
-                    grads_out.at[half, p_me, layer], arrived.at[layer, seat],
-                    grad_send, grad_recv.at[layer], half, me,
-                )
+
+    @pl.loop(0, features // CHUNK)
+    def _(c):
+        per = part // CHUNK
+        inner = pl.ds(pl.multiple_of(lax.rem(c, per) * CHUNK, CHUNK), CHUNK)
+        cols = pl.ds(pl.multiple_of(c * CHUNK, CHUNK), CHUNK)
+        gate = gate_a[:, cols].astype(F32)
+        value = (cot_a[:, cols].astype(F32) * gate * jax.nn.sigmoid(gate)).astype(BF16)
+        grad_memory[:, cols] = value
+        rows = contract(mix_tall[...], value, ((1,), (0,))).astype(BF16)
+        grads_out[c // per, :, :, :, inner] = rows.reshape(plane, LAYERS, ROW_LIMIT, CHUNK)
+
+    for k in range(LAYERS):
+        layer = need(k)
+        for hop in range(plane):
+            q = peer(hop)
+            for turn in range(sections):
+                if hop or turn:
+                    other = other_section(turn)
+                    remote(
+                        grads_out.at[other, q, layer], arrived.at[layer, seat],
+                        send, grad_recv.at[layer], other, at(z, q),
+                    )
+        pltpu.make_async_copy(
+            grads_out.at[sec, p_me, layer], arrived.at[layer, seat], grad_recv.at[layer]
+        ).start()
 
     drain(asked, ask_recv)
-    serving, summing = asked[sec * plane, :, :width], asked[0, :, width:]
+    served, summing = asked[sec * plane], asked[0]
     for q in range(1, plane):
-        serving = serving + asked[sec * plane + q, :, :width]
+        served = served + asked[sec * plane + q]
     for q in range(1, group):
-        summing = summing + asked[q, :, width:]
+        summing = summing + asked[q]
     for layer in range(LAYERS):
-        codes[layer, :, :width] = serving[layer : layer + 1]
-        codes[layer, :, width:] = summing[layer : layer + 1]
-
-    drain(asked_far, far_recv)
+        codes[layer] = served[layer : layer + 1]
+        codes_sum[layer] = summing[layer : layer + 1]
+
     for j, side in enumerate((x_side, y_side)):
-        serving = message[side, :, :width] + asked_far[j, :, :width]
+        served = message[side] + asked[group + j]
         for layer in range(LAYERS):
-            codes_aux[j, layer] = serving[layer : layer + 1]
+            codes_aux[j, layer] = served[layer : layer + 1]
 
     def lookup(code):
-        pick = (iota((rows_dev, width), 0).astype(F32) == code - 1.0).astype(F32)
-        return jnp.transpose(pick)[: plane * 2 * ROW_LIMIT].astype(BF16)
+        pick = (iota((rows_dev, code.shape[1]), 0).astype(F32) == code - 1.0).astype(F32)
+        return jnp.transpose(pick)[width : width + plane * 2 * ROW_LIMIT].astype(BF16)
 
     def look_aside(layer):
         return [lookup(codes_aux[j, layer]) for j in range(2)]
@@ -269,7 +271,7 @@
     def give(found, layer, c, q, column):
         remote(
             found.at[layer, q, :, strip(c)], fetched.at[column, layer, :, strip(c)],
-            row_send, row_recv.at[c], sec, at(z, q),
+            send, row_recv.at[c], sec, at(z, q),
         )
 
     def keep(found, layer, c, column):
@@ -278,11 +280,20 @@
             row_recv.at[c],
         ).start()
 
-    def serve(layer, pick, c, shared):
+    def shared(layer):
+        return (layer > 0) & (layer < last)
+
+    def serve(layer, pick, c, near):
         find(pick, col, rows_out, layer, c)
-        hops = [2 if c < PIECES // 2 else 1, *range(4, plane)] if shared else range(1, plane)
-        for hop in hops:
+        first = 2 if c < PIECES // 2 else 1
+        for hop in (first, *range(4, plane)):
             give(rows_out, layer, c, peer(hop), p_me)
+
+        @pl.when(~shared(layer) if near else z >= 0)
+        def _():
+            for hop in (3 - first, 3):
+                give(rows_out, layer, c, peer(hop), p_me)
+
         keep(rows_out, layer, c, p_me)
 
     def serve_aside(layer, picks, c):
@@ -293,70 +304,77 @@
         keep(rows_aux, layer, c, column)
 
     def summed(layer, cols):
-        code = codes[layer, :, width:][:, : group * ROW_LIMIT]
-        pick = hot(iota((rows_dev, group * ROW_LIMIT), 0).astype(F32) == code - 1.0)
-        block = arrived[layer, :, :, cols].reshape(group * ROW_LIMIT, -1)
+        code = codes_sum[layer][:, :width]
+        pick = hot(iota((rows_dev, width), 0).astype(F32) == code - 1.0)
+        block = arrived[layer, :, :, cols].reshape(width, -1)
         return contract(pick, block, ((1,), (0,)))
+
+    each = PIECES // HALVES
 
     def table_hop(h):
         behind, ahead = z - step_z * h, z + step_z * h
 
         @pl.when((behind >= 0) & (behind <= last))
         def _():
-            pick = lookup(codes[behind, :, :width])
-            for c in range(PIECES):
-                block = col.at[behind, :, pl.ds(c * piece, piece)]
-                drain(block, tab_recv.at[behind, c])
-
-                @pl.when(ahead_ok)
-                def _():
-                    remote(
-                        block, block, tab_send, tab_recv.at[behind, c],
-                        sec, at(z + step_z, p_me),
-                    )
-
-                remote(block, block, par_send, par_recv.at[behind, c], partner, me)
-                serve(behind, pick, c, h == 1)
+            pick = lookup(codes[behind])
+            for n in range(HALVES):
+                block = col.at[behind, :, half(n)]
+                drain(block, tab_recv.at[h - 1, n])
+
+                if h < last:
+
+                    @pl.when(ahead_ok)
+                    def _():
+                        remote(
+                            block, block, send, tab_recv.at[h, n], sec, at(z + step_z, p_me)
+                        )
+
+                remote(block, block, send, par_recv.at[h - 1, n], partner, me)
+                for c in range(n * each, (n + 1) * each):
+                    serve(behind, pick, c, h == 1)
 
         @pl.when((ahead >= 0) & (ahead <= last))
         def _():
-            pick = lookup(codes[ahead, :, :width])
-            for c in range(PIECES):
-                drain(col.at[ahead, :, pl.ds(c * piece, piece)], par_recv.at[ahead, c])
-                serve(ahead, pick, c, h == 1)
+            pick = lookup(codes[ahead])
+            for n in range(HALVES):
+                drain(col.at[ahead, :, half(n)], par_recv.at[h - 1, n])
+                for c in range(n * each, (n + 1) * each):
+                    serve(ahead, pick, c, h == 1)
 
     def own_aside():
+        drain(col.at[z, :, half(0)], aux_recv.at[0])
         for j in range(2):
-            c = 2 * j + parity
-            block = aux.at[z, :, strip(c)]
-            drain(block, aux_recv.at[z, c])
-            remote(block, block, par_send, aux_recv.at[z, c], partner, me)
+            block = aux.at[z, :, strip(2 * j + parity)]
+            remote(block, block, send, aux_recv.at[1], partner, me)
 
     def near_aside():
         behind, ahead = z - step_z, z + step_z
 
-        @pl.when((behind >= 0) & (behind <= last))
+        @pl.when(shared(behind))
         def _():
             picks = look_aside(behind)
-            for c in range(PIECES):
-                block = aux.at[behind, :, strip(c)]
-                drain(block, aux_recv.at[behind, c])
-                remote(block, block, par_send, aux_recv.at[behind, c], partner, me)
-                serve_aside(behind, picks, c)
-
-        @pl.when(ahead_ok)
+            for n in range(HALVES):
+                block = aux.at[behind, :, half(n)]
+                drain(block, aux_recv.at[2 + n])
+                remote(block, block, send, aux_recv.at[2 + HALVES + n], partner, me)
+                for c in range(n * each, (n + 1) * each):
+                    serve_aside(behind, picks, c)
+
+        @pl.when(shared(ahead))
         def _():
             picks = look_aside(ahead)
-            for c in range(PIECES):
-                drain(aux.at[ahead, :, strip(c)], aux_recv.at[ahead, c])
-                serve_aside(ahead, picks, c)
+            for n in range(HALVES):
+                drain(aux.at[ahead, :, half(n)], aux_recv.at[2 + HALVES + n])
+                for c in range(n * each, (n + 1) * each):
+                    serve_aside(ahead, picks, c)
 
     def reduce_step(k):
-        for way in range(2):
-            place = z if way == 0 else last - z
-            far = last - (k - place)
-            layer = far if way == 0 else last - far
-            target = z + 1 if way == 0 else z - 1
+        for turn in range(2):
+            way = jnp.where(z < LAYERS // 2, 1 - turn, turn)
+            up = way == 0
+            place = jnp.where(up, z, last - z)
+            layer = jnp.where(up, last - (k - place), k - place)
+            target = jnp.where(up, z + 1, z - 1)
 
             def pass_on(earlier):
                 for c in range(2):
@@ -369,7 +387,7 @@
                     rs_out[way, k, :, cols] = total.astype(BF16)
                     remote(
                         rs_out.at[way, k, :, cols], rs_in.at[way, k, :, cols],
-                        rs_send, rs_recv.at[way, k, c], sec, at(target, p_me),
+                        send, rs_recv.at[way, k, c], sec, at(target, p_me),
                     )
 
             @pl.when(place <= k)
@@ -387,23 +405,24 @@
                     pass_on(True)
 
     own_aside()
-    pick = lookup(codes[z, :, :width])
+    pick = lookup(codes[z])
     for c in range(PIECES):
-        serve(z, pick, c, True)
-    for j in range(2):
-        c = 2 * j + 1 - parity
-        drain(aux.at[z, :, strip(c)], aux_recv.at[z, c])
+        find(pick, col, rows_out, z, c)
+        for hop in (2 if c < PIECES // 2 else 1, *range(4, plane)):
+            give(rows_out, z, c, peer(hop), p_me)
+        keep(rows_out, z, c, p_me)
+    drain(col.at[z, :, half(0)], aux_recv.at[1])
     picks = look_aside(z)
     for c in range(PIECES):
         serve_aside(z, picks, c)
     reduce_step(0)
     table_hop(1)
 
-    @pl.when(ahead_ok)
+    @pl.when(ahead_ok & shared(z))
     def _():
-        for c in range(PIECES):
-            block = aux.at[z, :, strip(c)]
-            remote(block, block, tab_send, aux_recv.at[z, c], sec, at(z + step_z, p_me))
+        for n in range(HALVES):
+            block = aux.at[z, :, half(n)]
+            remote(block, block, send, aux_recv.at[2 + n], sec, at(z + step_z, p_me))
 
     mix_wide[:tokens] = contract(mixing_t[:, :tokens], wide_a, ((0,), (1,))).astype(BF16)
     mix_wide[tokens:] = contract(mixing_t[:, tokens:], wide_b, ((0,), (1,))).astype(BF16)
@@ -453,43 +472,52 @@
                 drain(rs_in.at[way, last - 1, :, cols], rs_recv.at[way, last - 1, c])
                 grad_table[:, cols] += rs_in[way, last - 1, :, cols].astype(F32)
 
-    drain(asked.at[pl.ds(0, group - 1)], ask_send)
-    drain(arrived.at[:, pl.ds(0, group - 1)], grad_send)
-    drain(asked_far, ask_send)
-    drain(rows_out.at[0, pl.ds(0, plane - 2)], row_send)
+    drain(asked.at[pl.ds(0, group + 1)], send)
+    drain(arrived.at[:, pl.ds(0, group - 1)], send)
+    drain(rows_out.at[0, pl.ds(0, plane - 2)], send)
     for c in range(2):
-        drain(col.at[z, :, strip(c)], tab_send)
-        drain(col.at[z, :, strip(c)], par_send)
+        drain(col.at[z, :, strip(c)], send)
+        drain(col.at[z, :, strip(c)], send)
 
     @pl.when(ahead_ok)
     def _():
-        drain(col.at[z], tab_send)
-        drain(col.at[z], tab_send)
+        drain(col.at[z], send)
+
+    @pl.when(ahead_ok & shared(z))
+    def _():
+        drain(col.at[z], send)
 
     for h in range(1, LAYERS):
         behind, ahead = z - step_z * h, z + step_z * h
 
         @pl.when((behind >= 0) & (behind <= last))
         def _():
-            drain(rows_out.at[0, pl.ds(0, plane - (2 if h == 1 else 1))], row_send)
-            drain(col.at[behind], par_send)
-            if h == 1:
-                drain(col.at[behind], par_send)
+            drain(col.at[behind], send)
 
             @pl.when(ahead_ok)
             def _():
-                drain(col.at[behind], tab_send)
-
-        @pl.when((ahead >= 0) & (ahead <= last))
-        def _():
-            drain(rows_out.at[0, pl.ds(0, plane - (2 if h == 1 else 1))], row_send)
+                drain(col.at[behind], send)
+
+        for layer in (behind, ahead):
+
+            @pl.when((layer >= 0) & (layer <= last))
+            def _():
+                drain(rows_out.at[0, pl.ds(0, plane - 2)], send)
+
+                @pl.when(~shared(layer) if h == 1 else z >= 0)
+                def _():
+                    drain(rows_out.at[0, pl.ds(0, 1)], send)
+
+    @pl.when(shared(z - step_z))
+    def _():
+        drain(col.at[z], send)
 
     for k in range(last):
         for way in range(2):
 
             @pl.when(k >= (z if way == 0 else last - z))
             def _():
-                drain(rs_out.at[way, k], rs_send)
+                drain(rs_out.at[way, k], send)
 
 
 def store(mixed_b, grad_gate, grad_weights, grad_table, *refs):
@@ -504,10 +532,6 @@
         copy.wait()
 
 
-def asked_width(group):
-    return -(-group * ROW_LIMIT // 128) * 128
-
-
 def local(gate_a, cotangent_a, gate_b, table, row_ids, slots, weights):
     owners = lax.axis_size("table")
     sections = lax.axis_size("section")
@@ -518,7 +542,7 @@
     listed = row_ids.shape[-1]
     picks = slots.shape[-1]
     part = features // sections
-    lanes = -(-plane * 2 * ROW_LIMIT // 128) * 128 + asked_width(group)
+    lanes = -(-(2 * plane + group) * ROW_LIMIT // 128) * 128
     slot_rows = owners * 2 * ROW_LIMIT
     vmem = pl.BlockSpec(memory_space=pltpu.VMEM)
     hbm = pl.BlockSpec(memory_space=pl.ANY)
@@ -531,12 +555,15 @@
             pltpu.VMEM((tokens, picks), F32),
             pltpu.VMEM((rows_dev, part), F32),
         ),
-        in_specs=[hbm] * 4 + [vmem] * 3,
+        in_specs=[hbm] * 7,
         out_specs=(vmem,) * 4,
         scratch_shapes=[
             pltpu.VMEM((tokens, features), BF16),
             pltpu.VMEM((tokens, features), BF16),
             pltpu.VMEM((tokens, features), BF16),
+            pltpu.VMEM((2, listed), jnp.int32),
+            pltpu.VMEM((2, tokens, picks), jnp.int32),
+            pltpu.VMEM((2, tokens, picks), F32),
             pltpu.VMEM((LAYERS, rows_dev, features), BF16),
             pltpu.VMEM((LAYERS, rows_dev, features), BF16),
             pltpu.VMEM((picks, 2 * tokens), F32),
@@ -545,10 +572,10 @@
             pltpu.VMEM((owners * ROW_LIMIT, tokens), BF16),
             pltpu.VMEM((slot_rows, listed), BF16),
             pltpu.VMEM((plane, LAYERS, lanes), F32),
-            pltpu.VMEM((group, LAYERS, lanes), F32),
-            pltpu.VMEM((2, LAYERS, lanes), F32),
+            pltpu.VMEM((group + 2, LAYERS, lanes), F32),
             pltpu.VMEM((LAYERS, 1, lanes), F32),
-            pltpu.VMEM((2, LAYERS, 1, lanes - asked_width(group)), F32),
+            pltpu.VMEM((LAYERS, 1, lanes), F32),
+            pltpu.VMEM((2, LAYERS, 1, lanes), F32),
             pltpu.VMEM((sections, plane, LAYERS, ROW_LIMIT, part), BF16),
             pltpu.VMEM((LAYERS, group, ROW_LIMIT, part), BF16),
             pltpu.VMEM((LAYERS, plane, 2 * ROW_LIMIT, features), BF16),
@@ -558,13 +585,15 @@
             pltpu.VMEM((tokens, slot_rows), F32),
             pltpu.VMEM((2, LAYERS - 1, rows_dev, part), BF16),
             pltpu.VMEM((2, LAYERS - 1, rows_dev, part), BF16),
-            dma((4,)),
-            dma, dma, dma,
-            dma, dma((LAYERS, PIECES)),
-            dma, dma((LAYERS, PIECES)), dma((LAYERS, PIECES)),
-            dma, dma((LAYERS,)),
-            dma, dma((PIECES,)),
-            dma, dma((2, LAYERS - 1, 2)),
+            dma((7,)),
+            dma,
+            dma,
+            dma((LAYERS - 1, HALVES)),
+            dma((LAYERS - 1, HALVES)),
+            dma((2 + 2 * HALVES,)),
+            dma((LAYERS,)),
+            dma((PIECES,)),
+            dma((2, LAYERS - 1, HALVES)),
         ],
         compiler_params=pltpu.CompilerParams(
             collective_id=0, has_side_effects=True, vmem_limit_bytes=60 * 1024 * 1024

time: 43.6 us -> 40.3 us (0.924)
  Pallas kernels: 42.8 us -> 39.5 us
    pallas_call x1, Pallas kernels: 41.6 us -> 38.3 us  [local(): pl.pallas_call(exchange, out_shape=(pltpu.VMEM((tokens, features), BF16),...]
where the time goes in v4:
time: 40.3 us; the launch traced here: 40.2 us
  Pallas kernels  39.5 us (98%)
  between operations  0.64 us (2%)
    pallas_call x1, Pallas kernels, local(): pl.pallas_call(exchange, out_shape=(pltpu.VMEM((tokens, features), BF16),...  38.3 us
    pallas_call x1, Pallas kernels, local(): pl.pallas_call(store, out_shape=tuple((jax.ShapeDtypeStruct(r.shape, r.dt...  1.19 us

profile of v4, /device:TPU:0, one launch (start us, length us, event | category | flops | bytes accessed | tf_op | source)
XLA Modules:
  0.0 40.2 jit_solution(14921012785046854545)
XLA Ops:
  0.6 38.3 %shard_map.102 = (bf16[64,4096]{1,0:T(8,128)(2,1)S(1)}, bf16[64,4096]{1,0:T(8,128)(2,1)S(1)}, f32[64,128]{1,0:T(8,128)S(1)}, f32[64,2048]{1,0:T(8,128)S(1)}) custom-call(bf16[64,4096]{1,0:T(8,128)(2,1)} %bitcast.9, bf16[64,4096]{1,0:T(8,128)(2,1)} %bitcast.10, bf16[64,4096]{1,0:T(8,128)(2,1)} %bitcast.11, bf16[64,4096]{1,0:T(8,128)(2,1)} %table_in.1, ...), custom_call_target="tpu_custom_call" | custom-call | tf_op jit(solution)/shard_map/pallas_call | solution.py:550
  39.0 1.2 %shard_map.103 = (bf16[64,4096]{1,0:T(8,128)(2,1)}, bf16[64,4096]{1,0:T(8,128)(2,1)}, f32[64,128]{1,0:T(8,128)}, f32[64,2048]{1,0:T(8,128)}) custom-call(bf16[64,4096]{1,0:T(8,128)(2,1)S(1)} %get-tuple-element.12.mixed_b, bf16[64,4096]{1,0:T(8,128)(2,1)S(1)} %get-tuple-element.13.grad_gate, f32[64,128]{1,0:T(8,128)S(1)} %get-tuple-element.14.grad_weights, ...), custom_call_target="tpu_custom_call" | custom-call | tf_op jit(solution)/shard_map/pallas_call | solution.py:605

commit v5 on v4

--- a/solution.py
+++ b/solution.py
@@ -9,7 +9,10 @@
 CHUNK = 512
 LAYERS = 4
 PIECES = 4
+PARTIAL = (1, 3)
+ORDER = (0, 2, 1, 3)
 HALVES = 2
+FAR_SHARE = 2
 UNROLL = 8
 MESH = pl.DeviceIdType.MESH
 BF16, F32 = jnp.bfloat16, jnp.float32
@@ -66,10 +69,10 @@
 
 def exchange(
     gate_a_in, cot_a_in, gate_b_in, table_in, row_ids_in, slots_in, weights_in,
-    mixed_b, grad_gate, grad_weights, grad_table,
-    gate_a, cot_a, gate_b, row_ids, slots, weights, col, aux, slots_t, weights_t, mix_wide, mix_tall, wide_list,
+    mixed_b, grad_gate, grad_table, scores, wide_list, slots,
+    gate_a, cot_a, gate_b, row_ids, weights, col, aux, slots_t, weights_t, mix_wide, mix_tall,
     message, asked, codes, codes_sum, codes_aux, grads_out, arrived, rows_out, rows_aux, fetched,
-    grad_memory, scores,
+    grad_memory,
     rs_out, rs_in,
     load, send, ask_recv, tab_recv, par_recv, aux_recv, grad_recv, row_recv, rs_recv,
 ):
@@ -83,6 +86,7 @@
     group = sections * plane
     width = group * ROW_LIMIT
     piece = features // PIECES
+    far = piece // FAR_SHARE
     last = LAYERS - 1
 
     sec = lax.axis_index("section")
@@ -262,46 +266,70 @@
     def look_aside(layer):
         return [lookup(codes_aux[j, layer]) for j in range(2)]
 
-    def find(pick, held, found, layer, c):
-        for k in range(piece // CHUNK):
-            cols = pl.ds(c * piece + k * CHUNK, CHUNK)
+    def span(block):
+        return pl.ds(*block[1:])
+
+    def whole(c):
+        return c, c * piece, piece
+
+    def tail(c):
+        return c, (c + 1) * piece - far, far
+
+    def find(pick, held, found, layer, block):
+        _, first, size = block
+        for k in range(0, size, CHUNK):
+            cols = pl.ds(first + k, min(CHUNK, size - k))
             rows = contract(pick, held[layer, :, cols], ((1,), (0,))).astype(BF16)
-            found[layer, :, :, cols] = rows.reshape(plane, 2 * ROW_LIMIT, CHUNK)
-
-    def give(found, layer, c, q, column):
+            found[layer, :, :, cols] = rows.reshape(plane, 2 * ROW_LIMIT, -1)
+
+    def give(found, layer, block, q, column):
+        cols = span(block)
         remote(
-            found.at[layer, q, :, strip(c)], fetched.at[column, layer, :, strip(c)],
-            send, row_recv.at[c], sec, at(z, q),
+            found.at[layer, q, :, cols], fetched.at[column, layer, :, cols],
+            send, row_recv.at[block[0]], sec, at(z, q),
         )
 
-    def keep(found, layer, c, column):
+    def keep(found, layer, block, column):
+        cols = span(block)
         pltpu.make_async_copy(
-            found.at[layer, p_me, :, strip(c)], fetched.at[column, layer, :, strip(c)],
-            row_recv.at[c],
+            found.at[layer, p_me, :, cols], fetched.at[column, layer, :, cols],
+            row_recv.at[block[0]],
         ).start()
 
-    def shared(layer):
+    def valid(layer):
+        return (layer >= 0) & (layer <= last)
+
+    def inner(layer):
         return (layer > 0) & (layer < last)
 
-    def serve(layer, pick, c, near):
-        find(pick, col, rows_out, layer, c)
+    def blocks(h, c):
+        if h == 0 or (h == 1 and c in PARTIAL):
+            return [(whole(c), True)]
+        if h == 2 and c in PARTIAL:
+            return [((c, c * piece, piece - far), False), (tail(c), None)]
+        return [(whole(c), None if h == 1 else False)]
+
+    def serve(layer, pick, c, h):
         first = 2 if c < PIECES // 2 else 1
-        for hop in (first, *range(4, plane)):
-            give(rows_out, layer, c, peer(hop), p_me)
-
-        @pl.when(~shared(layer) if near else z >= 0)
-        def _():
-            for hop in (3 - first, 3):
-                give(rows_out, layer, c, peer(hop), p_me)
-
-        keep(rows_out, layer, c, p_me)
-
-    def serve_aside(layer, picks, c):
-        j = 2 * c // PIECES
+        for block, shared in blocks(h, c):
+            find(pick, col, rows_out, layer, block)
+            for hop in (first, *range(4, plane)):
+                give(rows_out, layer, block, peer(hop), p_me)
+            if shared is not True:
+
+                @pl.when(~inner(layer) if shared is None else z >= 0)
+                def _():
+                    for hop in (3 - first, 3):
+                        give(rows_out, layer, block, peer(hop), p_me)
+
+            keep(rows_out, layer, block, p_me)
+
+    def serve_aside(layer, picks, block):
+        j = 2 * block[0] // PIECES
         column, target = ((x_side, y_side), (y_side, x_side))[j]
-        find(picks[j], aux, rows_aux, layer, c)
-        give(rows_aux, layer, c, target, column)
-        keep(rows_aux, layer, c, column)
+        find(picks[j], aux, rows_aux, layer, block)
+        give(rows_aux, layer, block, target, column)
+        keep(rows_aux, layer, block, column)
 
     def summed(layer, cols):
         code = codes_sum[layer][:, :width]
@@ -311,35 +339,40 @@
 
     each = PIECES // HALVES
 
-    def table_hop(h):
+    def pass_table(h, n):
+        behind = z - step_z * h
+
+        @pl.when(valid(behind))
+        def _():
+            block = col.at[behind, :, half(n)]
+            drain(block, tab_recv.at[h - 1, n])
+            if h < last:
+
+                @pl.when(ahead_ok)
+                def _():
+                    remote(block, block, send, tab_recv.at[h, n], sec, at(z + step_z, p_me))
+
+            remote(block, block, send, par_recv.at[h - 1, n], partner, me)
+
+    def serve_layer(h, passing):
         behind, ahead = z - step_z * h, z + step_z * h
 
-        @pl.when((behind >= 0) & (behind <= last))
+        @pl.when(valid(behind))
         def _():
             pick = lookup(codes[behind])
             for n in range(HALVES):
-                block = col.at[behind, :, half(n)]
-                drain(block, tab_recv.at[h - 1, n])
-
-                if h < last:
-
-                    @pl.when(ahead_ok)
-                    def _():
-                        remote(
-                            block, block, send, tab_recv.at[h, n], sec, at(z + step_z, p_me)
-                        )
-
-                remote(block, block, send, par_recv.at[h - 1, n], partner, me)
+                if passing:
+                    pass_table(h, n)
                 for c in range(n * each, (n + 1) * each):
-                    serve(behind, pick, c, h == 1)
-
-        @pl.when((ahead >= 0) & (ahead <= last))
+                    serve(behind, pick, c, h)
+
+        @pl.when(valid(ahead))
         def _():
             pick = lookup(codes[ahead])
             for n in range(HALVES):
                 drain(col.at[ahead, :, half(n)], par_recv.at[h - 1, n])
                 for c in range(n * each, (n + 1) * each):
-                    serve(ahead, pick, c, h == 1)
+                    serve(ahead, pick, c, h)
 
     def own_aside():
         drain(col.at[z, :, half(0)], aux_recv.at[0])
@@ -347,28 +380,59 @@
             block = aux.at[z, :, strip(2 * j + parity)]
             remote(block, block, send, aux_recv.at[1], partner, me)
 
-    def near_aside():
-        behind, ahead = z - step_z, z + step_z
-
-        @pl.when(shared(behind))
+    def landing(h, way, c):
+        if h == 1:
+            return 2 + way * PIECES + c
+        return 2 + 2 * PIECES + way * len(PARTIAL) + PARTIAL.index(c)
+
+    def near_aside(h):
+        behind, ahead = z - step_z * h, z + step_z * h
+
+        def each_block(layer, use):
+            for c in sorted(range(PIECES), key=lambda c: c not in PARTIAL):
+                for block, shared in blocks(h, c):
+                    if shared is True:
+                        use(block)
+                    elif shared is None:
+
+                        @pl.when(inner(layer))
+                        def _():
+                            use(block)
+
+        @pl.when(valid(behind))
         def _():
             picks = look_aside(behind)
-            for n in range(HALVES):
-                block = aux.at[behind, :, half(n)]
-                drain(block, aux_recv.at[2 + n])
-                remote(block, block, send, aux_recv.at[2 + HALVES + n], partner, me)
-                for c in range(n * each, (n + 1) * each):
-                    serve_aside(behind, picks, c)
-
-        @pl.when(shared(ahead))
+
+            def use(block):
+                c = block[0]
+                part = aux.at[behind, :, span(block)]
+                drain(part, aux_recv.at[landing(h, 0, c)])
+                if h == 1 and c in PARTIAL:
+
+                    @pl.when(inner(behind) & ahead_ok)
+                    def _():
+                        onward = aux.at[behind, :, span(tail(c))]
+                        remote(
+                            onward, onward, send, aux_recv.at[landing(2, 0, c)],
+                            sec, at(z + step_z, p_me),
+                        )
+
+                remote(part, part, send, aux_recv.at[landing(h, 1, c)], partner, me)
+                serve_aside(behind, picks, block)
+
+            each_block(behind, use)
+
+        @pl.when(valid(ahead))
         def _():
             picks = look_aside(ahead)
-            for n in range(HALVES):
-                drain(aux.at[ahead, :, half(n)], aux_recv.at[2 + HALVES + n])
-                for c in range(n * each, (n + 1) * each):
-                    serve_aside(ahead, picks, c)
-
-    def reduce_step(k):
+
+            def use(block):
+                drain(aux.at[ahead, :, span(block)], aux_recv.at[landing(h, 1, block[0])])
+                serve_aside(ahead, picks, block)
+
+            each_block(ahead, use)
+
+    def reduce_step(k, starts, follows):
         for turn in range(2):
             way = jnp.where(z < LAYERS // 2, 1 - turn, turn)
             up = way == 0
@@ -390,49 +454,64 @@
                         send, rs_recv.at[way, k, c], sec, at(target, p_me),
                     )
 
-            @pl.when(place <= k)
-            def _():
-                drain(arrived.at[layer], grad_recv.at[layer])
-
-            @pl.when(place == 0)
-            def _():
-                pass_on(False)
-
-            if k:
+            if starts:
+
+                @pl.when(place == 0)
+                def _():
+                    drain(arrived.at[layer], grad_recv.at[layer])
+                    pass_on(False)
+
+            if follows:
 
                 @pl.when((place > 0) & (place <= k))
                 def _():
+                    drain(arrived.at[layer], grad_recv.at[layer])
                     pass_on(True)
 
     own_aside()
     pick = lookup(codes[z])
     for c in range(PIECES):
-        find(pick, col, rows_out, z, c)
-        for hop in (2 if c < PIECES // 2 else 1, *range(4, plane)):
-            give(rows_out, z, c, peer(hop), p_me)
-        keep(rows_out, z, c, p_me)
+        serve(z, pick, c, 0)
+    pass_table(1, 0)
     drain(col.at[z, :, half(0)], aux_recv.at[1])
     picks = look_aside(z)
     for c in range(PIECES):
-        serve_aside(z, picks, c)
-    reduce_step(0)
-    table_hop(1)
-
-    @pl.when(ahead_ok & shared(z))
+        serve_aside(z, picks, whole(c))
+    for n in range(1, HALVES):
+        pass_table(1, n)
+
+    def pass_aside(c):
+        block = aux.at[z, :, strip(c)]
+        remote(block, block, send, aux_recv.at[landing(1, 0, c)], sec, at(z + step_z, p_me))
+
+    @pl.when(ahead_ok)
     def _():
-        for n in range(HALVES):
-            block = aux.at[z, :, half(n)]
-            remote(block, block, send, aux_recv.at[2 + n], sec, at(z + step_z, p_me))
+        for c in PARTIAL:
+            pass_aside(c)
+
+    @pl.when(ahead_ok & inner(z))
+    def _():
+        for c in range(PIECES):
+            if c not in PARTIAL:
+                pass_aside(c)
+
+    reduce_step(0, True, False)
+    serve_layer(1, False)
 
     mix_wide[:tokens] = contract(mixing_t[:, :tokens], wide_a, ((0,), (1,))).astype(BF16)
     mix_wide[tokens:] = contract(mixing_t[:, tokens:], wide_b, ((0,), (1,))).astype(BF16)
     scores[...] = jnp.zeros_like(scores)
 
-    for h in range(2, LAYERS):
-        table_hop(h)
-        reduce_step(h - 1)
-        if h == 2:
-            near_aside()
+    serve_layer(2, True)
+    reduce_step(1, True, True)
+    for k in range(2, last):
+        reduce_step(k, True, False)
+    near_aside(1)
+    for h in range(3, LAYERS):
+        serve_layer(h, True)
+    near_aside(2)
+    for k in range(2, last):
+        reduce_step(k, False, True)
 
     drain(arrived.at[z], grad_recv.at[z])
 
@@ -442,8 +521,8 @@
         grad_table[:, cols] = summed(z, cols)
 
     drain(gate_b, load.at[3])
-    for c in range(PIECES):
-        drain(fetched.at[:, :, :, pl.ds(c * piece, piece)], row_recv.at[c])
+    for c in ORDER:
+        drain(fetched.at[:, :, :, strip(c)], row_recv.at[c])
         for k in range(piece // CHUNK):
             cols = pl.ds(c * piece + k * CHUNK, CHUNK)
             rows = fetched[:, :, :, cols].reshape(owners * 2 * ROW_LIMIT, CHUNK)
@@ -458,11 +537,6 @@
             gate = gate_b[:, cols].astype(F32)
             mixed_b[:, cols] = (gate * jax.nn.sigmoid(gate) * memory[tokens:]).astype(BF16)
 
-    found = contract(
-        scores[...], wide_list[...].astype(F32), ((1,), (0,)), precision=lax.Precision.HIGHEST
-    )
-    grad_weights[...] = jnp.take_along_axis(found, slots[0], axis=1)
-
     for way in range(2):
 
         @pl.when((z > 0) if way == 0 else (z < last))
@@ -482,15 +556,16 @@
     @pl.when(ahead_ok)
     def _():
         drain(col.at[z], send)
-
-    @pl.when(ahead_ok & shared(z))
+        drain(col.at[z, :, half(0)], send)
+
+    @pl.when(ahead_ok & inner(z))
     def _():
-        drain(col.at[z], send)
+        drain(col.at[z, :, half(0)], send)
 
     for h in range(1, LAYERS):
         behind, ahead = z - step_z * h, z + step_z * h
 
-        @pl.when((behind >= 0) & (behind <= last))
+        @pl.when(valid(behind))
         def _():
             drain(col.at[behind], send)
 
@@ -498,19 +573,34 @@
             def _():
                 drain(col.at[behind], send)
 
+            for c in range(PIECES):
+                for block, shared in blocks(h, c):
+                    if shared is True:
+                        drain(aux.at[z, :, span(block)], send)
+                    elif shared is None:
+
+                        @pl.when(inner(behind))
+                        def _():
+                            drain(aux.at[z, :, span(block)], send)
+
+                if h == 1 and c in PARTIAL:
+
+                    @pl.when(inner(behind) & ahead_ok)
+                    def _():
+                        drain(aux.at[z, :, span(tail(c))], send)
+
         for layer in (behind, ahead):
 
-            @pl.when((layer >= 0) & (layer <= last))
+            @pl.when(valid(layer))
             def _():
                 drain(rows_out.at[0, pl.ds(0, plane - 2)], send)
-
-                @pl.when(~shared(layer) if h == 1 else z >= 0)
-                def _():
-                    drain(rows_out.at[0, pl.ds(0, 1)], send)
-
-    @pl.when(shared(z - step_z))
-    def _():
-        drain(col.at[z], send)
+                for c in range(PIECES):
+                    for block, shared in blocks(h, c):
+                        if shared is not True:
+
+                            @pl.when(~inner(layer) if shared is None else z >= 0)
+                            def _():
+                                drain(rows_out.at[0, 0, :, span(block)], send)
 
     for k in range(last):
         for way in range(2):
@@ -520,14 +610,21 @@
                 drain(rs_out.at[way, k], send)
 
 
-def store(mixed_b, grad_gate, grad_weights, grad_table, *refs):
-    outs, sems = refs[:4], refs[4]
+def store(mixed_b, grad_gate, grad_table, scores, wide_list, slots, *refs):
+    outs, grad_weights, sems = refs[:4], refs[4], refs[5]
     copies = [
         pltpu.make_async_copy(source, target, sems.at[n])
-        for n, (source, target) in enumerate(zip((mixed_b, grad_gate, grad_weights, grad_table), outs))
+        for n, (source, target) in enumerate(
+            zip((mixed_b, grad_gate, grad_table, grad_weights), outs)
+        )
     ]
-    for copy in copies:
+    for copy in copies[:3]:
         copy.start()
+    found = contract(
+        scores[...], wide_list[...].astype(F32), ((1,), (0,)), precision=lax.Precision.HIGHEST
+    )
+    grad_weights[...] = jnp.take_along_axis(found, slots[0], axis=1)
+    copies[3].start()
     for copy in copies:
         copy.wait()
 
@@ -547,22 +644,23 @@
     vmem = pl.BlockSpec(memory_space=pltpu.VMEM)
     hbm = pl.BlockSpec(memory_space=pl.ANY)
     dma = pltpu.SemaphoreType.DMA
-    mixed_b, grad_gate, grad_weights, grad_table = pl.pallas_call(
+    results = pl.pallas_call(
         exchange,
         out_shape=(
             pltpu.VMEM((tokens, features), BF16),
             pltpu.VMEM((tokens, features), BF16),
-            pltpu.VMEM((tokens, picks), F32),
             pltpu.VMEM((rows_dev, part), F32),
+            pltpu.VMEM((tokens, slot_rows), F32),
+            pltpu.VMEM((slot_rows, listed), BF16),
+            pltpu.VMEM((2, tokens, picks), jnp.int32),
         ),
         in_specs=[hbm] * 7,
-        out_specs=(vmem,) * 4,
+        out_specs=(vmem,) * 6,
         scratch_shapes=[
             pltpu.VMEM((tokens, features), BF16),
             pltpu.VMEM((tokens, features), BF16),
             pltpu.VMEM((tokens, features), BF16),
             pltpu.VMEM((2, listed), jnp.int32),
-            pltpu.VMEM((2, tokens, picks), jnp.int32),
             pltpu.VMEM((2, tokens, picks), F32),
             pltpu.VMEM((LAYERS, rows_dev, features), BF16),
             pltpu.VMEM((LAYERS, rows_dev, features), BF16),
@@ -570,7 +668,6 @@
             pltpu.VMEM((picks, 2 * tokens), F32),
             pltpu.VMEM((2 * tokens, slot_rows), BF16),
             pltpu.VMEM((owners * ROW_LIMIT, tokens), BF16),
-            pltpu.VMEM((slot_rows, listed), BF16),
             pltpu.VMEM((plane, LAYERS, lanes), F32),
             pltpu.VMEM((group + 2, LAYERS, lanes), F32),
             pltpu.VMEM((LAYERS, 1, lanes), F32),
@@ -582,7 +679,6 @@
             pltpu.VMEM((LAYERS, plane, 2 * ROW_LIMIT, features), BF16),
             pltpu.VMEM((plane, LAYERS, 2 * ROW_LIMIT, features), BF16),
             pltpu.VMEM((tokens, features), BF16),
-            pltpu.VMEM((tokens, slot_rows), F32),
             pltpu.VMEM((2, LAYERS - 1, rows_dev, part), BF16),
             pltpu.VMEM((2, LAYERS - 1, rows_dev, part), BF16),
             dma((7,)),
@@ -590,7 +686,7 @@
             dma,
             dma((LAYERS - 1, HALVES)),
             dma((LAYERS - 1, HALVES)),
-            dma((2 + 2 * HALVES,)),
+            dma((2 + 2 * PIECES + 2 * len(PARTIAL),)),
             dma((LAYERS,)),
             dma((PIECES,)),
             dma((2, LAYERS - 1, HALVES)),
@@ -601,13 +697,17 @@
     )(
         gate_a[0], cotangent_a[0], gate_b[0], table, row_ids[0, :, 0], slots[0], weights[0]
     )
-    results = (mixed_b, grad_gate, grad_weights, grad_table)
-    mixed_b, grad_gate, grad_weights, grad_table = pl.pallas_call(
+    mixed_b, grad_gate, grad_table, grad_weights = pl.pallas_call(
         store,
-        out_shape=tuple(jax.ShapeDtypeStruct(r.shape, r.dtype) for r in results),
-        in_specs=[vmem] * 4,
+        out_shape=(
+            jax.ShapeDtypeStruct((tokens, features), BF16),
+            jax.ShapeDtypeStruct((tokens, features), BF16),
+            jax.ShapeDtypeStruct((rows_dev, part), F32),
+            jax.ShapeDtypeStruct((tokens, picks), F32),
+        ),
+        in_specs=[vmem] * 6,
         out_specs=(hbm,) * 4,
-        scratch_shapes=[dma((4,))],
+        scratch_shapes=[pltpu.VMEM((tokens, picks), F32), dma((4,))],
     )(*(pltpu.with_memory_space_constraint(r, pltpu.VMEM) for r in results))
     return mixed_b[None], grad_gate[None], grad_weights[None], grad_table
 

time: 40.3 us -> 39.3 us (0.975)
  Pallas kernels: 39.5 us -> 38.5 us
    pallas_call x1, Pallas kernels: 38.3 us -> 37.3 us  [local(): pl.pallas_call(exchange, out_shape=(pltpu.VMEM((tokens, features), BF16),...]
where the time goes in v5:
time: 39.3 us; the launch traced here: 39.1 us
  Pallas kernels  38.5 us (98%)
  between operations  0.64 us (2%)
    pallas_call x1, Pallas kernels, local(): pl.pallas_call(exchange, out_shape=(pltpu.VMEM((tokens, features), BF16),...  37.3 us
    pallas_call x1, Pallas kernels, local(): pl.pallas_call(store, out_shape=(jax.ShapeDtypeStruct((tokens, features),...  1.19 us

profile of v5, /device:TPU:0, one launch (start us, length us, event | category | flops | bytes accessed | tf_op | source)
XLA Modules:
  0.0 39.1 jit_solution(15030446252799329271)
XLA Ops:
  0.6 37.3 %shard_map.102 = (bf16[64,4096]{1,0:T(8,128)(2,1)S(1)}, bf16[64,4096]{1,0:T(8,128)(2,1)S(1)}, f32[64,2048]{1,0:T(8,128)S(1)}, f32[64,256]{1,0:T(8,128)S(1)}, bf1...) custom-call(bf16[64,4096]{1,0:T(8,128)(2,1)} %bitcast.9, bf16[64,4096]{1,0:T(8,128)(2,1)} %bitcast.10, ...), custom_call_target="tpu_custom_call" | custom-call | tf_op jit(solution)/shard_map/pallas_call | solution.py:647
  37.9 1.2 %shard_map.103 = (bf16[64,4096]{1,0:T(8,128)(2,1)}, bf16[64,4096]{1,0:T(8,128)(2,1)}, f32[64,2048]{1,0:T(8,128)}, f32[64,128]{1,0:T(8,128)}) custom-call(bf16[64,4096]{1,0:T(8,128)(2,1)S(1)} %get-tuple-element.14.mixed_b, bf16[64,4096]{1,0:T(8,128)(2,1)S(1)} %get-tuple-element.15.grad_gate, f32[64,2048]{1,0:T(8,128)S(1)} %get-tuple-element.16.grad_table, ...), custom_call_target="tpu_custom_call" | custom-call | tf_op jit(solution)/shard_map/pallas_call | solution.py:700

commit v6 on v5

--- a/solution.py
+++ b/solution.py
@@ -12,7 +12,7 @@
 PARTIAL = (1, 3)
 ORDER = (0, 2, 1, 3)
 HALVES = 2
-FAR_SHARE = 2
+FAR_EIGHTHS = 5
 UNROLL = 8
 MESH = pl.DeviceIdType.MESH
 BF16, F32 = jnp.bfloat16, jnp.float32
@@ -63,6 +63,25 @@
     return lax.fori_loop(0, picks // UNROLL, group, start)
 
 
+def finish(c, gate_a, cot_a, gate_b, fetched, mix_wide, grad_memory, mixed_b, grad_gate, scores):
+    tokens, features = gate_a.shape
+    slot_rows = mix_wide.shape[1]
+    piece = features // PIECES
+    for k in range(piece // CHUNK):
+        cols = pl.ds(c * piece + k * CHUNK, CHUNK)
+        rows = fetched[:, :, :, cols].reshape(slot_rows, CHUNK)
+        memory = contract(mix_wide[...], rows, ((1,), (0,)))
+        gate = gate_a[:, cols].astype(F32)
+        sig = jax.nn.sigmoid(gate)
+        incoming = cot_a[:, cols].astype(F32)
+        grad_gate[:, cols] = (
+            incoming * memory[:tokens] * sig * (1.0 + gate * (1.0 - sig))
+        ).astype(BF16)
+        scores[...] += contract(grad_memory[:, cols], rows, ((1,), (1,)))
+        gate = gate_b[:, cols].astype(F32)
+        mixed_b[:, cols] = (gate * jax.nn.sigmoid(gate) * memory[tokens:]).astype(BF16)
+
+
 def drain(block, sem):
     pltpu.make_async_copy(block, block, sem).wait()
 
@@ -70,9 +89,9 @@
 def exchange(
     gate_a_in, cot_a_in, gate_b_in, table_in, row_ids_in, slots_in, weights_in,
     mixed_b, grad_gate, grad_table, scores, wide_list, slots,
-    gate_a, cot_a, gate_b, row_ids, weights, col, aux, slots_t, weights_t, mix_wide, mix_tall,
-    message, asked, codes, codes_sum, codes_aux, grads_out, arrived, rows_out, rows_aux, fetched,
-    grad_memory,
+    gate_a, cot_a, gate_b, fetched, mix_wide, grad_memory,
+    row_ids, weights, col, aux, slots_t, weights_t, mix_tall,
+    message, asked, codes, codes_sum, codes_aux, grads_out, arrived, rows_out, rows_aux,
     rs_out, rs_in,
     load, send, ask_recv, tab_recv, par_recv, aux_recv, grad_recv, row_recv, rs_recv,
 ):
@@ -86,7 +105,7 @@
     group = sections * plane
     width = group * ROW_LIMIT
     piece = features // PIECES
-    far = piece // FAR_SHARE
+    far = FAR_EIGHTHS * piece // 8
     last = LAYERS - 1
 
     sec = lax.axis_index("section")
@@ -521,21 +540,9 @@
         grad_table[:, cols] = summed(z, cols)
 
     drain(gate_b, load.at[3])
-    for c in ORDER:
+    for c in ORDER[:-1]:
         drain(fetched.at[:, :, :, strip(c)], row_recv.at[c])
-        for k in range(piece // CHUNK):
-            cols = pl.ds(c * piece + k * CHUNK, CHUNK)
-            rows = fetched[:, :, :, cols].reshape(owners * 2 * ROW_LIMIT, CHUNK)
-            memory = contract(mix_wide[...], rows, ((1,), (0,)))
-            gate = gate_a[:, cols].astype(F32)
-            sig = jax.nn.sigmoid(gate)
-            incoming = cot_a[:, cols].astype(F32)
-            grad_gate[:, cols] = (
-                incoming * memory[:tokens] * sig * (1.0 + gate * (1.0 - sig))
-            ).astype(BF16)
-            scores[...] += contract(grad_memory[:, cols], rows, ((1,), (1,)))
-            gate = gate_b[:, cols].astype(F32)
-            mixed_b[:, cols] = (gate * jax.nn.sigmoid(gate) * memory[tokens:]).astype(BF16)
+        finish(c, gate_a, cot_a, gate_b, fetched, mix_wide, grad_memory, mixed_b, grad_gate, scores)
 
     for way in range(2):
 
@@ -546,6 +553,7 @@
                 drain(rs_in.at[way, last - 1, :, cols], rs_recv.at[way, last - 1, c])
                 grad_table[:, cols] += rs_in[way, last - 1, :, cols].astype(F32)
 
+    drain(fetched.at[:, :, :, strip(ORDER[-1])], row_recv.at[ORDER[-1]])
     drain(asked.at[pl.ds(0, group + 1)], send)
     drain(arrived.at[:, pl.ds(0, group - 1)], send)
     drain(rows_out.at[0, pl.ds(0, plane - 2)], send)
@@ -610,21 +618,36 @@
                 drain(rs_out.at[way, k], send)
 
 
-def store(mixed_b, grad_gate, grad_table, scores, wide_list, slots, *refs):
-    outs, grad_weights, sems = refs[:4], refs[4], refs[5]
+def store(
+    mixed_b, grad_gate, grad_table, scores, wide_list, slots,
+    gate_a, cot_a, gate_b, fetched, mix_wide, grad_memory,
+    mixed_out, grad_gate_out, grad_table_out, grad_weights_out, grad_weights, sems,
+):
+    features = gate_a.shape[1]
+    done = pl.ds(0, features - features // PIECES)
+    rest = pl.ds(features - features // PIECES, features // PIECES)
+
+    def put(source, target, n):
+        copy = pltpu.make_async_copy(source, target, sems.at[n])
+        copy.start()
+        return copy
+
     copies = [
-        pltpu.make_async_copy(source, target, sems.at[n])
-        for n, (source, target) in enumerate(
-            zip((mixed_b, grad_gate, grad_table, grad_weights), outs)
-        )
+        put(mixed_b.at[:, done], mixed_out.at[:, done], 0),
+        put(grad_gate.at[:, done], grad_gate_out.at[:, done], 1),
+        put(grad_table, grad_table_out, 2),
     ]
-    for copy in copies[:3]:
-        copy.start()
+    finish(
+        ORDER[-1], gate_a, cot_a, gate_b, fetched, mix_wide, grad_memory,
+        mixed_b, grad_gate, scores,
+    )
+    copies.append(put(mixed_b.at[:, rest], mixed_out.at[:, rest], 3))
+    copies.append(put(grad_gate.at[:, rest], grad_gate_out.at[:, rest], 4))
     found = contract(
         scores[...], wide_list[...].astype(F32), ((1,), (0,)), precision=lax.Precision.HIGHEST
     )
     grad_weights[...] = jnp.take_along_axis(found, slots[0], axis=1)
-    copies[3].start()
+    copies.append(put(grad_weights, grad_weights_out, 5))
     for copy in copies:
         copy.wait()
 
@@ -653,20 +676,22 @@
             pltpu.VMEM((tokens, slot_rows), F32),
             pltpu.VMEM((slot_rows, listed), BF16),
             pltpu.VMEM((2, tokens, picks), jnp.int32),
-        ),
-        in_specs=[hbm] * 7,
-        out_specs=(vmem,) * 6,
-        scratch_shapes=[
             pltpu.VMEM((tokens, features), BF16),
             pltpu.VMEM((tokens, features), BF16),
             pltpu.VMEM((tokens, features), BF16),
+            pltpu.VMEM((plane, LAYERS, 2 * ROW_LIMIT, features), BF16),
+            pltpu.VMEM((2 * tokens, slot_rows), BF16),
+            pltpu.VMEM((tokens, features), BF16),
+        ),
+        in_specs=[pl.BlockSpec(memory_space=pltpu.HBM)] * 7,
+        out_specs=(vmem,) * 12,
+        scratch_shapes=[
             pltpu.VMEM((2, listed), jnp.int32),
             pltpu.VMEM((2, tokens, picks), F32),
             pltpu.VMEM((LAYERS, rows_dev, features), BF16),
             pltpu.VMEM((LAYERS, rows_dev, features), BF16),
             pltpu.VMEM((picks, 2 * tokens), F32),
             pltpu.VMEM((picks, 2 * tokens), F32),
-            pltpu.VMEM((2 * tokens, slot_rows), BF16),
             pltpu.VMEM((owners * ROW_LIMIT, tokens), BF16),
             pltpu.VMEM((plane, LAYERS, lanes), F32),
             pltpu.VMEM((group + 2, LAYERS, lanes), F32),
@@ -677,8 +702,6 @@
             pltpu.VMEM((LAYERS, group, ROW_LIMIT, part), BF16),
             pltpu.VMEM((LAYERS, plane, 2 * ROW_LIMIT, features), BF16),
             pltpu.VMEM((LAYERS, plane, 2 * ROW_LIMIT, features), BF16),
-            pltpu.VMEM((plane, LAYERS, 2 * ROW_LIMIT, features), BF16),
-            pltpu.VMEM((tokens, features), BF16),
             pltpu.VMEM((2, LAYERS - 1, rows_dev, part), BF16),
             pltpu.VMEM((2, LAYERS - 1, rows_dev, part), BF16),
             dma((7,)),
@@ -692,10 +715,15 @@
             dma((2, LAYERS - 1, HALVES)),
         ],
         compiler_params=pltpu.CompilerParams(
-            collective_id=0, has_side_effects=True, vmem_limit_bytes=60 * 1024 * 1024
+            collective_id=0, has_side_effects=True, vmem_limit_bytes=44 * 1024 * 1024
         ),
     )(
-        gate_a[0], cotangent_a[0], gate_b[0], table, row_ids[0, :, 0], slots[0], weights[0]
+        *(
+            pltpu.with_memory_space_constraint(x, pltpu.HBM)
+            for x in (
+                gate_a[0], cotangent_a[0], gate_b[0], table, row_ids[0, :, 0], slots[0], weights[0]
+            )
+        )
     )
     mixed_b, grad_gate, grad_table, grad_weights = pl.pallas_call(
         store,
@@ -705,9 +733,10 @@
             jax.ShapeDtypeStruct((rows_dev, part), F32),
             jax.ShapeDtypeStruct((tokens, picks), F32),
         ),
-        in_specs=[vmem] * 6,
+        in_specs=[vmem] * 12,
         out_specs=(hbm,) * 4,
-        scratch_shapes=[pltpu.VMEM((tokens, picks), F32), dma((4,))],
+        scratch_shapes=[pltpu.VMEM((tokens, picks), F32), dma((6,))],
+        compiler_params=pltpu.CompilerParams(vmem_limit_bytes=8 * 1024 * 1024),
     )(*(pltpu.with_memory_space_constraint(r, pltpu.VMEM) for r in results))
     return mixed_b[None], grad_gate[None], grad_weights[None], grad_table
 

time: 39.3 us -> 38.8 us (0.987)
  Pallas kernels: 38.5 us -> 38 us
    pallas_call x1, Pallas kernels: 37.3 us -> 36.6 us  [local(): pl.pallas_call(exchange, out_shape=(pltpu.VMEM((tokens, features), BF16),...]
where the time goes in v6:
time: 38.8 us; the launch traced here: 38.7 us
  Pallas kernels  38 us (98%)
  between operations  0.64 us (2%)
    pallas_call x1, Pallas kernels, local(): pl.pallas_call(exchange, out_shape=(pltpu.VMEM((tokens, features), BF16),...  36.6 us
    pallas_call x1, Pallas kernels, local(): pl.pallas_call(store, out_shape=(jax.ShapeDtypeStruct((tokens, features),...  1.4 us

profile of v6, /device:TPU:0, one launch (start us, length us, event | category | flops | bytes accessed | tf_op | source)
XLA Modules:
  0.0 38.7 jit_solution(2669786976371439958)
XLA Ops:
  0.6 36.6 %shard_map.102 = (bf16[64,4096]{1,0:T(8,128)(2,1)S(1)}, bf16[64,4096]{1,0:T(8,128)(2,1)S(1)}, f32[64,2048]{1,0:T(8,128)S(1)}, f32[64,256]{1,0:T(8,128)S(1)}, bf1...) custom-call(bf16[64,4096]{1,0:T(8,128)(2,1)} %bitcast.9, ...), custom_call_target="tpu_custom_call" | custom-call | tf_op jit(solution)/shard_map/pallas_call | solution.py:670
  37.3 1.4 %shard_map.103 = (bf16[64,4096]{1,0:T(8,128)(2,1)}, bf16[64,4096]{1,0:T(8,128)(2,1)}, f32[64,2048]{1,0:T(8,128)}, f32[64,128]{1,0:T(8,128)}) custom-call(bf16[64,4096]{1,0:T(8,128)(2,1)S(1)} %get-tuple-element.20.mixed_b, bf16[64,4096]{1,0:T(8,128)(2,1)S(1)} %get-tuple-element.21.grad_gate, f32[64,2048]{1,0:T(8,128)S(1)} %get-tuple-element.22.grad_table, ...), custom_call_target="tpu_custom_call" | custom-call | tf_op jit(solution)/shard_map/pallas_call | solution.py:728

commit v7 on v6

--- a/solution.py
+++ b/solution.py
@@ -88,9 +88,9 @@
 
 def exchange(
     gate_a_in, cot_a_in, gate_b_in, table_in, row_ids_in, slots_in, weights_in,
-    mixed_b, grad_gate, grad_table, scores, wide_list, slots,
+    mixed_b, grad_gate, grad_table, scores, spots,
     gate_a, cot_a, gate_b, fetched, mix_wide, grad_memory,
-    row_ids, weights, col, aux, slots_t, weights_t, mix_tall,
+    row_ids, slots, weights, col, aux, slots_t, weights_t, mix_tall,
     message, asked, codes, codes_sum, codes_aux, grads_out, arrived, rows_out, rows_aux,
     rs_out, rs_in,
     load, send, ask_recv, tab_recv, par_recv, aux_recv, grad_recv, row_recv, rs_recv,
@@ -231,7 +231,6 @@
     wide_a = hot(space == spot_a * (2 * ROW_LIMIT) + rank_a)
     wide_b = hot(space == spot_b * (2 * ROW_LIMIT) + (rank_b + ROW_LIMIT))
     tall_a = hot(iota((owners * ROW_LIMIT, listed), 0) == spot_a * ROW_LIMIT + rank_a)
-    wide_list[...] = wide_a
     mix_tall[...] = contract(tall_a, mixing_t[:, :tokens], ((1,), (0,))).astype(BF16)
 
     drain(gate_a, load.at[1])
@@ -503,29 +502,31 @@
         block = aux.at[z, :, strip(c)]
         remote(block, block, send, aux_recv.at[landing(1, 0, c)], sec, at(z + step_z, p_me))
 
-    @pl.when(ahead_ok)
+    @pl.when(ahead_ok & inner(z))
+    def _():
+        for c in sorted(range(PIECES), key=lambda c: c not in PARTIAL):
+            pass_aside(c)
+
+    reduce_step(0, True, False)
+
+    @pl.when(ahead_ok & ~inner(z))
     def _():
         for c in PARTIAL:
             pass_aside(c)
 
-    @pl.when(ahead_ok & inner(z))
-    def _():
-        for c in range(PIECES):
-            if c not in PARTIAL:
-                pass_aside(c)
-
-    reduce_step(0, True, False)
     serve_layer(1, False)
 
     mix_wide[:tokens] = contract(mixing_t[:, :tokens], wide_a, ((0,), (1,))).astype(BF16)
     mix_wide[tokens:] = contract(mixing_t[:, tokens:], wide_b, ((0,), (1,))).astype(BF16)
     scores[...] = jnp.zeros_like(scores)
+    place_a = jnp.broadcast_to(spot_a * (2 * ROW_LIMIT) + rank_a, (tokens, listed))
+    spots[...] = jnp.take_along_axis(place_a, slots[0], axis=1)
 
     serve_layer(2, True)
     reduce_step(1, True, True)
+    near_aside(1)
     for k in range(2, last):
         reduce_step(k, True, False)
-    near_aside(1)
     for h in range(3, LAYERS):
         serve_layer(h, True)
     near_aside(2)
@@ -619,7 +620,7 @@
 
 
 def store(
-    mixed_b, grad_gate, grad_table, scores, wide_list, slots,
+    mixed_b, grad_gate, grad_table, scores, spots,
     gate_a, cot_a, gate_b, fetched, mix_wide, grad_memory,
     mixed_out, grad_gate_out, grad_table_out, grad_weights_out, grad_weights, sems,
 ):
@@ -643,10 +644,17 @@
     )
     copies.append(put(mixed_b.at[:, rest], mixed_out.at[:, rest], 3))
     copies.append(put(grad_gate.at[:, rest], grad_gate_out.at[:, rest], 4))
-    found = contract(
-        scores[...], wide_list[...].astype(F32), ((1,), (0,)), precision=lax.Precision.HIGHEST
-    )
-    grad_weights[...] = jnp.take_along_axis(found, slots[0], axis=1)
+    picks = grad_weights.shape[1]
+    where = spots[...]
+    found = jnp.zeros(grad_weights.shape, F32)
+    for first in range(0, scores.shape[1], picks):
+        near = where - first
+        inside = (near >= 0) & (near < picks)
+        got = jnp.take_along_axis(
+            scores[:, first : first + picks], jnp.where(inside, near, 0), axis=1
+        )
+        found = jnp.where(inside, got, found)
+    grad_weights[...] = found
     copies.append(put(grad_weights, grad_weights_out, 5))
     for copy in copies:
         copy.wait()
@@ -674,8 +682,7 @@
             pltpu.VMEM((tokens, features), BF16),
             pltpu.VMEM((rows_dev, part), F32),
             pltpu.VMEM((tokens, slot_rows), F32),
-            pltpu.VMEM((slot_rows, listed), BF16),
-            pltpu.VMEM((2, tokens, picks), jnp.int32),
+            pltpu.VMEM((tokens, picks), jnp.int32),
             pltpu.VMEM((tokens, features), BF16),
             pltpu.VMEM((tokens, features), BF16),
             pltpu.VMEM((tokens, features), BF16),
@@ -684,9 +691,10 @@
             pltpu.VMEM((tokens, features), BF16),
         ),
         in_specs=[pl.BlockSpec(memory_space=pltpu.HBM)] * 7,
-        out_specs=(vmem,) * 12,
+        out_specs=(vmem,) * 11,
         scratch_shapes=[
             pltpu.VMEM((2, listed), jnp.int32),
+            pltpu.VMEM((2, tokens, picks), jnp.int32),
             pltpu.VMEM((2, tokens, picks), F32),
             pltpu.VMEM((LAYERS, rows_dev, features), BF16),
             pltpu.VMEM((LAYERS, rows_dev, features), BF16),
@@ -733,7 +741,7 @@
             jax.ShapeDtypeStruct((rows_dev, part), F32),
             jax.ShapeDtypeStruct((tokens, picks), F32),
         ),
-        in_specs=[vmem] * 12,
+        in_specs=[vmem] * 11,
         out_specs=(hbm,) * 4,
         scratch_shapes=[pltpu.VMEM((tokens, picks), F32), dma((6,))],
         compiler_params=pltpu.CompilerParams(vmem_limit_bytes=8 * 1024 * 1024),

time: 38.8 us -> 38.6 us (level)
  no operation moved by 1% of the time
where the time goes in v7:
time: 38.6 us; the launch traced here: 38.4 us
  Pallas kernels  37.8 us (98%)
  between operations  0.64 us (2%)
    pallas_call x1, Pallas kernels, local(): pl.pallas_call(exchange, out_shape=(pltpu.VMEM((tokens, features), BF16),...  36.6 us
    pallas_call x1, Pallas kernels, local(): pl.pallas_call(store, out_shape=(jax.ShapeDtypeStruct((tokens, features),...  1.21 us

profile of v7, /device:TPU:0, one launch (start us, length us, event | category | flops | bytes accessed | tf_op | source)
XLA Modules:
  0.0 38.4 jit_solution(13453534540596512171)
XLA Ops:
  0.6 36.6 %shard_map.102 = (bf16[64,4096]{1,0:T(8,128)(2,1)S(1)}, bf16[64,4096]{1,0:T(8,128)(2,1)S(1)}, f32[64,2048]{1,0:T(8,128)S(1)}, f32[64,256]{1,0:T(8,128)S(1)}, s32...) custom-call(bf16[64,4096]{1,0:T(8,128)(2,1)} %bitcast.9, ...), custom_call_target="tpu_custom_call" | custom-call | tf_op jit(solution)/shard_map/pallas_call | solution.py:678
  37.2 1.2 %shard_map.103 = (bf16[64,4096]{1,0:T(8,128)(2,1)}, bf16[64,4096]{1,0:T(8,128)(2,1)}, f32[64,2048]{1,0:T(8,128)}, f32[64,128]{1,0:T(8,128)}) custom-call(bf16[64,4096]{1,0:T(8,128)(2,1)S(1)} %get-tuple-element.19.mixed_b, bf16[64,4096]{1,0:T(8,128)(2,1)S(1)} %get-tuple-element.20.grad_gate, f32[64,2048]{1,0:T(8,128)S(1)} %get-tuple-element.21.grad_table, ...), custom_call_target="tpu_custom_call" | custom-call | tf_op jit(solution)/shard_map/pallas_call | solution.py:736

commit v8 on v7

--- a/solution.py
+++ b/solution.py
@@ -12,7 +12,7 @@
 PARTIAL = (1, 3)
 ORDER = (0, 2, 1, 3)
 HALVES = 2
-FAR_EIGHTHS = 5
+FAR_EIGHTHS = 6
 UNROLL = 8
 MESH = pl.DeviceIdType.MESH
 BF16, F32 = jnp.bfloat16, jnp.float32
@@ -94,6 +94,7 @@
     message, asked, codes, codes_sum, codes_aux, grads_out, arrived, rows_out, rows_aux,
     rs_out, rs_in,
     load, send, ask_recv, tab_recv, par_recv, aux_recv, grad_recv, row_recv, rs_recv,
+    corner_in,
 ):
     sections = lax.axis_size("section")
     owners = lax.axis_size("table")
@@ -159,7 +160,7 @@
 
     for hop in range(plane):
         for turn in range(sections):
-            if hop or turn:
+            if (hop or turn) and hop != 3:
                 greet(other_section(turn), at(z, peer(hop)))
 
     @pl.when(z > 0)
@@ -190,17 +191,25 @@
     for q in range(plane):
         message[q] = asking[q * LAYERS : (q + 1) * LAYERS]
 
-    signals = group - 1 + jnp.where(z > 0, 1, 0) + jnp.where(z < last, 1, 0)
+    signals = group - 1 - sections + jnp.where(z > 0, 1, 0) + jnp.where(z < last, 1, 0)
     pl.semaphore_wait(pltpu.get_barrier_semaphore(), signals)
-
-    for hop in range(plane):
-        q = peer(hop)
-        for turn in range(sections):
-            if hop or turn:
-                remote(
-                    message.at[q], asked.at[seat], send, ask_recv,
-                    other_section(turn), at(z, q),
-                )
+    for side in (x_side, y_side):
+        pl.semaphore_signal(
+            corner_in, inc=1,
+            device_id={"section": sec, "table": at(z, side)}, device_id_type=MESH,
+        )
+
+    def ask(hops):
+        for hop in hops:
+            q = peer(hop)
+            for turn in range(sections):
+                if hop or turn:
+                    remote(
+                        message.at[q], asked.at[seat], send, ask_recv,
+                        other_section(turn), at(z, q),
+                    )
+
+    ask([hop for hop in range(plane) if hop != 3])
     pltpu.make_async_copy(message.at[p_me], asked.at[seat], ask_recv).start()
 
     for j, side in enumerate((x_side, y_side)):
@@ -233,6 +242,8 @@
     tall_a = hot(iota((owners * ROW_LIMIT, listed), 0) == spot_a * ROW_LIMIT + rank_a)
     mix_tall[...] = contract(tall_a, mixing_t[:, :tokens], ((1,), (0,))).astype(BF16)
 
+    pl.semaphore_wait(corner_in, 2)
+    ask([3])
     drain(gate_a, load.at[1])
     drain(cot_a, load.at[2])
 
@@ -262,21 +273,6 @@
             grads_out.at[sec, p_me, layer], arrived.at[layer, seat], grad_recv.at[layer]
         ).start()
 
-    drain(asked, ask_recv)
-    served, summing = asked[sec * plane], asked[0]
-    for q in range(1, plane):
-        served = served + asked[sec * plane + q]
-    for q in range(1, group):
-        summing = summing + asked[q]
-    for layer in range(LAYERS):
-        codes[layer] = served[layer : layer + 1]
-        codes_sum[layer] = summing[layer : layer + 1]
-
-    for j, side in enumerate((x_side, y_side)):
-        served = message[side] + asked[group + j]
-        for layer in range(LAYERS):
-            codes_aux[j, layer] = served[layer : layer + 1]
-
     def lookup(code):
         pick = (iota((rows_dev, code.shape[1]), 0).astype(F32) == code - 1.0).astype(F32)
         return jnp.transpose(pick)[width : width + plane * 2 * ROW_LIMIT].astype(BF16)
@@ -487,10 +483,26 @@
                     pass_on(True)
 
     own_aside()
+    pass_table(1, 0)
+
+    drain(asked, ask_recv)
+    served, summing = asked[sec * plane], asked[0]
+    for q in range(1, plane):
+        served = served + asked[sec * plane + q]
+    for q in range(1, group):
+        summing = summing + asked[q]
+    for layer in range(LAYERS):
+        codes[layer] = served[layer : layer + 1]
+        codes_sum[layer] = summing[layer : layer + 1]
+
+    for j, side in enumerate((x_side, y_side)):
+        served = message[side] + asked[group + j]
+        for layer in range(LAYERS):
+            codes_aux[j, layer] = served[layer : layer + 1]
+
     pick = lookup(codes[z])
     for c in range(PIECES):
         serve(z, pick, c, 0)
-    pass_table(1, 0)
     drain(col.at[z, :, half(0)], aux_recv.at[1])
     picks = look_aside(z)
     for c in range(PIECES):
@@ -721,6 +733,7 @@
             dma((LAYERS,)),
             dma((PIECES,)),
             dma((2, LAYERS - 1, HALVES)),
+            pltpu.SemaphoreType.REGULAR,
         ],
         compiler_params=pltpu.CompilerParams(
             collective_id=0, has_side_effects=True, vmem_limit_bytes=44 * 1024 * 1024

time: 38.6 us -> 38.3 us (level)
  no operation moved by 1% of the time
where the time goes in v8:
time: 38.3 us; the launch traced here: 38.2 us
  Pallas kernels  37.5 us (98%)
  between operations  0.64 us (2%)
    pallas_call x1, Pallas kernels, local(): pl.pallas_call(exchange, out_shape=(pltpu.VMEM((tokens, features), BF16),...  36.3 us
    pallas_call x1, Pallas kernels, local(): pl.pallas_call(store, out_shape=(jax.ShapeDtypeStruct((tokens, features),...  1.21 us

profile of v8, /device:TPU:0, one launch (start us, length us, event | category | flops | bytes accessed | tf_op | source)
XLA Modules:
  0.0 38.2 jit_solution(16931921402443272756)
XLA Ops:
  0.6 36.3 %shard_map.102 = (bf16[64,4096]{1,0:T(8,128)(2,1)S(1)}, bf16[64,4096]{1,0:T(8,128)(2,1)S(1)}, f32[64,2048]{1,0:T(8,128)S(1)}, f32[64,256]{1,0:T(8,128)S(1)}, s32...) custom-call(bf16[64,4096]{1,0:T(8,128)(2,1)} %bitcast.9, ...), custom_call_target="tpu_custom_call" | custom-call | tf_op jit(solution)/shard_map/pallas_call | solution.py:690
  37.0 1.2 %shard_map.103 = (bf16[64,4096]{1,0:T(8,128)(2,1)}, bf16[64,4096]{1,0:T(8,128)(2,1)}, f32[64,2048]{1,0:T(8,128)}, f32[64,128]{1,0:T(8,128)}) custom-call(bf16[64,4096]{1,0:T(8,128)(2,1)S(1)} %get-tuple-element.19.mixed_b, bf16[64,4096]{1,0:T(8,128)(2,1)S(1)} %get-tuple-element.20.grad_gate, f32[64,2048]{1,0:T(8,128)S(1)} %get-tuple-element.21.grad_table, ...), custom_call_target="tpu_custom_call" | custom-call | tf_op jit(solution)/shard_map/pallas_call | solution.py:749

commit v9 on v8

--- a/solution.py
+++ b/solution.py
@@ -13,7 +13,7 @@
 ORDER = (0, 2, 1, 3)
 HALVES = 2
 FAR_EIGHTHS = 6
-UNROLL = 8
+UNROLL = 16
 MESH = pl.DeviceIdType.MESH
 BF16, F32 = jnp.bfloat16, jnp.float32
 

time: 38.3 us -> 38.3 us (level)
  no operation moved by 1% of the time
where the time goes in v9:
time: 38.3 us; the launch traced here: 38.2 us
  Pallas kernels  37.5 us (98%)
  between operations  0.64 us (2%)
    pallas_call x1, Pallas kernels, local(): pl.pallas_call(exchange, out_shape=(pltpu.VMEM((tokens, features), BF16),...  36.3 us
    pallas_call x1, Pallas kernels, local(): pl.pallas_call(store, out_shape=(jax.ShapeDtypeStruct((tokens, features),...  1.21 us

profile of v9, /device:TPU:0, one launch (start us, length us, event | category | flops | bytes accessed | tf_op | source)
XLA Modules:
  0.0 38.2 jit_solution(13389207507296625085)
XLA Ops:
  0.6 36.3 %shard_map.102 = (bf16[64,4096]{1,0:T(8,128)(2,1)S(1)}, bf16[64,4096]{1,0:T(8,128)(2,1)S(1)}, f32[64,2048]{1,0:T(8,128)S(1)}, f32[64,256]{1,0:T(8,128)S(1)}, s32...) custom-call(bf16[64,4096]{1,0:T(8,128)(2,1)} %bitcast.9, ...), custom_call_target="tpu_custom_call" | custom-call | tf_op jit(solution)/shard_map/pallas_call | solution.py:690
  37.0 1.2 %shard_map.103 = (bf16[64,4096]{1,0:T(8,128)(2,1)}, bf16[64,4096]{1,0:T(8,128)(2,1)}, f32[64,2048]{1,0:T(8,128)}, f32[64,128]{1,0:T(8,128)}) custom-call(bf16[64,4096]{1,0:T(8,128)(2,1)S(1)} %get-tuple-element.19.mixed_b, bf16[64,4096]{1,0:T(8,128)(2,1)S(1)} %get-tuple-element.20.grad_gate, f32[64,2048]{1,0:T(8,128)S(1)} %get-tuple-element.21.grad_table, ...), custom_call_target="tpu_custom_call" | custom-call | tf_op jit(solution)/shard_map/pallas_call | solution.py:749
